TPU v7x, 32 devices: a whole 2x2x4 slice. The times are simulated.
32 devices in a mesh: group: 2 (over x), wide: 16 (over z, y, core).
Axes of the slice: x: 2, y: 2, z: 4, core: 2. Of those that a mesh axis runs over, the one named last changes fastest.
Arguments:
- tokens: bfloat16 [192, 2688], P('group', 'wide'), parts along dimension 0, may hold values from -6 to 6
- mix_gain: bfloat16 [2688], replicated, may hold values from 0.099609375 to 1.8984375
- proj_inner: bfloat16 [2688, 2, 4096], P(None, None, 'wide'), may hold values from -0.125 to 0.125
- proj_maps: bfloat16 [2688, 2048], P(None, 'wide'), may hold values from -0.125 to 0.125
- proj_step: bfloat16 [2688, 64], P(None, 'wide'), may hold values from -0.125 to 0.125
- window_inner: bfloat16 [192, 3, 4096], P('group', None, 'wide'), parts along dimension 0, may hold values from -6 to 6
- window_maps: bfloat16 [192, 3, 2048], P('group', None, 'wide'), parts along dimension 0, may hold values from -6 to 6
- kernel_inner: bfloat16 [4, 4096], P(None, 'wide'), may hold values from -3 to 3
- kernel_maps: bfloat16 [4, 2048], P(None, 'wide'), may hold values from -3 to 3
- step_bias: float32 [64], P('wide'), may hold values from -4 to -1
- decay_log: float32 [64], P('wide'), may hold values from -1 to 2.5
- skip_gain: float32 [64], P('wide'), may hold values from 0.5 to 2
- gated_gain: bfloat16 [4096], P('wide'), may hold values from 0.099609375 to 1.8984375
- proj_out: bfloat16 [4096, 2688], P('wide'), may hold values from -0.125 to 0.125
- ssm_state: float32 [192, 64, 64, 128], P('group', 'wide'), parts along dimension 0, may hold values from -0.6 to 0.6
- moe_gain: bfloat16 [2688], replicated, may hold values from 0.099609375 to 1.8984375
- router_weight: bfloat16 [2688, 16], replicated, may hold values from -0.125 to 0.125
- expert_ids: int32 [192, 6], P('group'), parts along dimension 0, may hold values from 0 to 15, all different within a row; in each aligned block of 96 rows (0 to 95, 96 to 191, ...) at most 96 rows name the same one
- expert_up: bfloat16 [16, 2688, 928], P('wide'), may hold values from -0.125 to 0.125
- expert_down: bfloat16 [16, 928, 2688], P('wide'), may hold values from -0.1875 to 0.1875
Outputs:
- next_hidden: bfloat16 [192, 2688], P('group', 'wide'), parts along dimension 0
- new_state: float32 [192, 64, 64, 128], P('group', 'wide'), parts along dimension 0
There are 2 independent parts, one for each index of `group`. A program takes and returns all parts, laid end to end along the dimension named above; an argument that names none is the same for every part. Nothing has to cross between parts.
Inputs may be any that keep to these rules, and one draw needn't show every extreme that they name: `expert_ids`: each token names 6 different experts; no expert is named by more than 96 tokens of a part, a bound that some block reaches.
All inputs are finite; a program needn't handle non-finite values.
Results may differ from a plain program's by a relative error of at most 0.013.
Values may be sent and summed in bfloat16 or wider, within the bound.
A program may use at most 128 MiB of HBM per device.

v0:
```python
import jax
import jax.numpy as jnp
from jax import lax
from jax.sharding import PartitionSpec as P

WIDTH = 2688
HEADS = 64
HEAD_DIM = 64
STATE = 128
GROUPS = 8
TOPK = 6
INNER = 4096


epsilon = 1e-05


def rms_scale(values, axis):
    return lax.rsqrt(jnp.mean(values * values, axis=axis, keepdims=True) + epsilon)


def convolve(window, fresh, kernel):
    stacked = jnp.concatenate([window, fresh[:, None, :]], axis=1).astype(jnp.float32)
    mixed = jnp.sum(stacked * kernel.astype(jnp.float32)[None], axis=1)
    return jax.nn.silu(mixed).astype(jnp.bfloat16)


def expert_rows(rows, upward, downward):
    hidden_units = jnp.dot(rows, upward, preferred_element_type=jnp.float32)
    active = jnp.square(jnp.maximum(hidden_units, 0.0)).astype(jnp.bfloat16)
    return jnp.dot(active, downward, preferred_element_type=jnp.float32).astype(jnp.bfloat16)


def route_gates(logits, expert_ids):
    onehot = (
        expert_ids[:, :, None] == jnp.arange(logits.shape[1], dtype=jnp.int32)[None, None, :]
    ).astype(jnp.float32)
    chosen = jnp.sum(onehot * logits[:, None, :], axis=2)
    score = jax.nn.sigmoid(chosen)
    return score / jnp.sum(score, axis=1, keepdims=True)


def slot_codes(expert_ids, experts, capacity):
    flat = expert_ids.reshape(-1)
    onehot = (flat[:, None] == jnp.arange(experts, dtype=jnp.int32)[None, :]).astype(jnp.int32)
    before = jnp.cumsum(onehot, axis=0) - onehot
    slots = jnp.sum(before * onehot, axis=1)
    return (flat * capacity + slots).reshape(expert_ids.shape)


def slot_tables(codes, gates, count):
    targets = jnp.arange(count, dtype=jnp.int32)
    match = codes[None, :, :] == targets[:, None, None]
    pick = jnp.any(match, axis=2).astype(jnp.bfloat16)
    weigh = jnp.sum(jnp.where(match, gates[None], 0.0), axis=2)
    return (pick, weigh)


def local(
    tokens,
    mix_gain,
    proj_inner,
    proj_maps,
    proj_step,
    window_inner,
    window_maps,
    kernel_inner,
    kernel_maps,
    step_bias,
    decay_log,
    skip_gain,
    gated_gain,
    proj_out,
    ssm_state,
    moe_gain,
    router_weight,
    expert_ids,
    expert_up,
    expert_down,
):
    devices = lax.axis_size("wide")
    device = lax.axis_index("wide")
    seqs = tokens.shape[0]
    slice_width = tokens.shape[1]
    capacity = min(seqs, 4 * seqs * TOPK // devices)
    full_tokens = lax.all_gather(tokens, "wide", axis=1, tiled=True)
    tokens_float = full_tokens.astype(jnp.float32)
    normed = (tokens_float * rms_scale(tokens_float, 1) * mix_gain.astype(jnp.float32)).astype(
        jnp.bfloat16
    )
    local_inner = proj_inner.shape[2]
    inner = jnp.dot(
        normed, proj_inner.reshape(WIDTH, 2 * local_inner), preferred_element_type=jnp.float32
    ).astype(jnp.bfloat16)
    gate_input = inner[:, :local_inner]
    raw_inner = inner[:, local_inner:]
    maps_raw = jnp.dot(normed, proj_maps, preferred_element_type=jnp.float32).astype(jnp.bfloat16)
    step_raw = jnp.dot(normed, proj_step, preferred_element_type=jnp.float32).astype(jnp.bfloat16)
    conv_inner = convolve(window_inner, raw_inner, kernel_inner)
    conv_maps = convolve(window_maps, maps_raw, kernel_maps)
    all_maps = lax.all_gather(conv_maps, "wide", axis=1, tiled=True)
    local_heads = proj_step.shape[1]
    group = device * local_heads // (HEADS // GROUPS)
    in_maps = lax.dynamic_slice_in_dim(all_maps, group * STATE, STATE, 1).astype(jnp.float32)
    out_maps = lax.dynamic_slice_in_dim(all_maps, GROUPS * STATE + group * STATE, STATE, 1).astype(
        jnp.float32
    )
    step_size = jax.nn.softplus(step_raw.astype(jnp.float32) + step_bias)
    decay = jnp.exp(-jnp.exp(decay_log) * step_size)
    head_inputs = conv_inner.astype(jnp.float32).reshape(seqs, local_heads, HEAD_DIM)
    driven = (step_size[:, :, None] * head_inputs)[..., None] * in_maps[:, None, None, :]
    new_state = decay[:, :, None, None] * ssm_state + driven
    readout = (
        jnp.einsum("shpn,sn->shp", new_state, out_maps, precision=lax.Precision.HIGHEST)
        + skip_gain[None, :, None] * head_inputs
    )
    gated = readout.reshape(seqs, local_inner) * jax.nn.silu(gate_input.astype(jnp.float32))
    group_mask = (jnp.arange(GROUPS, dtype=jnp.int32) == group).astype(jnp.float32)
    partial_squares = jnp.sum(gated * gated, axis=1)[:, None] * group_mask[None, :]
    group_squares = lax.psum(partial_squares, "wide")
    own_squares = jnp.sum(group_squares * group_mask[None, :], axis=1, keepdims=True)
    norm_scale = lax.rsqrt(own_squares / (INNER // GROUPS) + epsilon)
    gated_out = (gated * norm_scale * gated_gain.astype(jnp.float32)).astype(jnp.bfloat16)
    mixer_terms = jnp.dot(gated_out, proj_out, preferred_element_type=jnp.float32)
    codes = slot_codes(expert_ids, devices, capacity)
    mixer_slice = lax.psum_scatter(mixer_terms, "wide", scatter_dimension=1, tiled=True)
    hidden_round = (tokens.astype(jnp.float32) + mixer_slice).astype(jnp.bfloat16)
    hidden_slice = lax.optimization_barrier(hidden_round).astype(jnp.float32)
    gain_slice = lax.dynamic_slice_in_dim(moe_gain, device * slice_width, slice_width, 0).astype(
        jnp.float32
    )
    router_slice = lax.dynamic_slice_in_dim(
        router_weight, device * slice_width, slice_width, 0
    ).astype(jnp.float32)
    weighted = hidden_slice * gain_slice
    squares, part_logits = lax.psum(
        (
            jnp.sum(hidden_slice * hidden_slice, axis=1),
            jnp.dot(weighted, router_slice, precision=lax.Precision.HIGHEST),
        ),
        "wide",
    )
    moe_scale = lax.rsqrt(squares[:, None] / WIDTH + epsilon)
    gates = route_gates(part_logits * moe_scale, expert_ids)
    moe_input = (hidden_slice * moe_scale * gain_slice).astype(jnp.bfloat16)
    pick, weigh = slot_tables(codes, gates, devices * capacity)
    sent = (
        jnp.dot(pick, moe_input, preferred_element_type=jnp.float32)
        .astype(jnp.bfloat16)
        .reshape(devices, capacity, slice_width)
    )
    served = expert_rows(
        lax.all_to_all(sent, "wide", split_axis=0, concat_axis=2, tiled=True)[0],
        expert_up[0],
        expert_down[0],
    )
    returned = lax.all_to_all(served[None], "wide", split_axis=2, concat_axis=0, tiled=True)
    moe_slice = jnp.dot(
        weigh.T,
        returned.reshape(devices * capacity, slice_width).astype(jnp.float32),
        precision=lax.Precision.HIGHEST,
    )
    next_hidden = (hidden_slice + moe_slice).astype(jnp.bfloat16)
    return (next_hidden, new_state)


def solution(mesh):
    in_specs = (
        P("group", "wide"),
        P(),
        P(None, None, "wide"),
        P(None, "wide"),
        P(None, "wide"),
        P("group", None, "wide"),
        P("group", None, "wide"),
        P(None, "wide"),
        P(None, "wide"),
        P("wide"),
        P("wide"),
        P("wide"),
        P("wide"),
        P("wide", None),
        P("group", "wide", None, None),
        P(),
        P(),
        P("group", None),
        P("wide", None, None),
        P("wide", None, None),
    )
    out_specs = (P("group", "wide"), P("group", "wide", None, None))
    return jax.shard_map(local, mesh=mesh, in_specs=in_specs, out_specs=out_specs, check_vma=False)
```

profile of v0, /device:TPU:0, one launch (start us, length us, event | category | flops | bytes accessed | tf_op | source)
XLA Modules:
  0.0 292.7 jit_solution(6536486973410003831)
XLA Ops:
  7.2 0.0 copy-start
  7.2 0.0 reduce-scatter.4.cloned.1.call-start
  7.3 0.0 copy-start.2
  7.3 25.6 %all_gather.6 = bf16[96,2688]{0,1:T(8,128)(2,1)S(1)} all-gather(bf16[96,168]{0,1:T(8,128)(2,1)} %param.20), channel_id=1, replica_groups=mesh['group'=2,'wide'=16] {'wide'}, dimensions={1}, use_global_device_ids=true | all-gather | bytes 548352 | tf_op jit(solution)/shard_map/all_gather | solution.py:86
  32.9 0.4 fusion.11
  33.3 0.7 convert_element_type.109
  34.0 0.7 convert_element_type.120
  34.6 1.8 fusion.24
  36.6 18.5 %all_gather.7 = bf16[96,2048]{1,0:T(8,128)(2,1)S(1)} all-gather(bf16[96,128]{1,0:T(8,128)(2,1)S(1)} %multiply_convert_fusion.3), channel_id=1, replica_groups=mesh['group'=2,'wide'=16] {'wide'}, dimensions={1}, use_global_device_ids=true | all-gather | bytes 417792 | tf_op jit(solution)/shard_map/all_gather | solution.py:101
  55.1 0.5 copy.88
  55.6 0.0 copy-start.10
  55.6 0.0 copy-start.9
  55.6 1.2 convolution_convert_fusion.1
  56.9 0.1 copy.71
  57.0 0.5 multiply_exponential_fusion
  57.6 0.1 convert_multiply_fusion.3
  57.6 0.1 copy.72
  57.8 0.1 copy.70
  57.9 7.0 %multiply_add_fusion = f32[96,4,64,128]{3,2,1,0:T(8,128)S(1)} fusion(f32[96,4,64,128]{3,2,1,0:T(8,128)} %param.34, f32[96,128]{1,0:T(8,128)S(1)} %get-tuple-element.5, f32[96,4,64]{2,1,0:T(4,128)S(1)} %copy.72, f32[96,4]{1,0:T(8,128)S(1)} %copy.70), kind=kLoop, calls=%fused_computation | loop fusion | flops 9437184 | bytes 25314816 | tf_op jit(solution)/shard_map/add | solution.py:112
  64.9 0.0 copy-start.1
  64.9 4.8 %copy-done.1 = f32[96,4,64,128]{3,2,1,0:T(8,128)} copy-done((f32[96,4,64,128]{3,2,1,0:T(8,128)}, f32[96,4,64,128]{3,2,1,0:T(8,128)S(1)}, u32[]{:S(2)}) %copy-start.1) | copy-done | bytes 12582936
  69.7 14.7 %fusion.40 = f32[96,1,4,64]{3,1,2,0:T(1,128)S(1)} fusion(f32[96,4,64,128]{3,2,1,0:T(8,128)S(1)} %multiply_add_fusion, bf16[96,128,1,1]{1,0,2,3:T(8,128)(2,1)S(1)} %get-tuple-element.4), kind=kOutput, calls=%fused_computation.52 | convolution fusion | flops 37748736 | bytes 12705792 | tf_op jit(solution)/shard_map/shpn,sn->shp/dot_general | solution.py:114
  84.4 0.1 copy.84
  84.5 0.0 copy-done.8
  84.5 0.1 fusion.30
  84.6 0.0 copy-start.3
  84.6 0.1 copy.73
  84.7 0.1 multiply_reduce_fusion.2
  84.8 0.1 broadcast_multiply_fusion.1
  84.9 31.1 %psum.21 = f32[96,8]{0,1:T(8,128)S(1)} all-reduce(f32[96,8]{0,1:T(8,128)S(1)} %broadcast_multiply_fusion.1), channel_id=1, replica_groups=mesh['group'=2,'wide'=16] {'wide'}, use_global_device_ids=true, to_apply=%region_4.5 | all-reduce | flops 768 | bytes 6144 | tf_op jit(solution)/shard_map/psum | solution.py:120
  116.0 0.1 multiply_reduce_fusion.3
  116.1 1.8 fusion.39
  117.9 0.0 reduce-scatter.4.cloned.1.call-update
  117.9 0.1 copy.74
  118.0 0.1 eq.60
  118.2 1.7 reduce-window.6
  119.9 0.2 slice_reduce_fusion
  120.1 0.1 bitcast_bitcast_fusion
  120.2 0.1 reduce_sum.101
  120.4 0.1 copy.77
  120.4 0.8 dynamic-slice_convert_fusion.1
  121.2 0.6 fusion.4
  121.9 50.8 %reduce-scatter.4.cloned.1.call-done = f32[96,168]{0,1:T(8,128)} async-done(((f32[96,2688]{0,1:T(8,128)}), f32[96,168]{0,1:T(8,128)}) %reduce-scatter.4.cloned.1.call-update) | async-done | bytes 64528
  172.7 0.9 add_convert_fusion
  173.6 0.9 fusion.35
  174.5 30.5 %all-reduce.2 = (f32[96,16]{0,1:T(8,128)S(1)}, f32[96]{0:T(128)S(1)}) all-reduce(f32[96,16]{0,1:T(8,128)S(1)} %fusion.35, f32[96]{0:T(128)S(1)} %fusion.36), channel_id=1, replica_groups=mesh['group'=2,'wide'=16] {'wide'}, use_global_device_ids=true, to_apply=%region_10.11 | all-reduce | flops 1632 | bytes 13056 | tf_op jit(solution)/shard_map/psum | solution.py:136
  205.0 0.3 convolution_convert_fusion
  205.4 0.6 reshape.115
  205.9 0.2 copy.78
  206.1 21.2 %all_to_all.30 = bf16[16,96,168]{1,2,0:T(8,128)(2,1)S(1)} all-to-all(bf16[16,96,168]{1,2,0:T(8,128)(2,1)S(1)} %copy.78), channel_id=1, replica_groups=mesh['group'=2,'wide'=16] {'wide'}, dimensions={0} | all-to-all | bytes 1032192 | tf_op jit(solution)/shard_map/all_to_all | solution.py:153
  227.4 6.5 %fusion.8 = bf16[1,96,2688]{2,1,0:T(8,128)(2,1)S(1)} fusion(bf16[1,928,2688]{2,1,0:T(8,128)(2,1)} %param.39, bf16[96,2688]{0,1:T(8,128)(2,1)S(1)} %bitcast.74, bf16[1,2688,928]{1,2,0:T(8,128)(2,1)} %param.38), kind=kOutput, calls=%fused_computation.9 | convolution fusion | flops 958399488 | bytes 11010048 | tf_op jit(solution)/shard_map/dot_general | solution.py:31
  233.9 1.9 copy.80
  235.8 0.5 broadcast.123
  236.3 14.9 %reduce.2 = bf16[2688,96]{1,0:T(8,128)(2,1)S(1)} reduce(bf16[2688,1,96]{2,1,0:T(2,128)(2,1)S(1)} %bitcast.70, bf16[]{:T(256)} %broadcast.123), dimensions={1}, to_apply=%bitcast.55.reduce_sub_computation | reduce | bytes 1032194
  251.3 1.9 reshape.122
  253.2 4.5 %all-to-all-start.1 = ((bf16[16,2,8064]{2,1,0:T(2,128)(2,1)}), bf16[16,2,8064]{2,1,0:T(2,128)(2,1)}, u32[]{:S(2)}, u32[]{:S(2)}) async-start(bf16[16,2,8064]{2,1,0:T(2,128)(2,1)} %reshape.122), calls=%async_computation.1 | async-start | bytes 1032192 | tf_op jit(solution)/shard_map/all_to_all | solution.py:157
  257.8 0.5 select_reduce_fusion
  258.3 13.3 %all-to-all-done.1 = bf16[16,2,8064]{2,1,0:T(2,128)(2,1)} async-done(((bf16[16,2,8064]{2,1,0:T(2,128)(2,1)}), bf16[16,2,8064]{2,1,0:T(2,128)(2,1)}, u32[]{:S(2)}, u32[]{:S(2)}) %all-to-all-start.1) | async-done | bytes 516128 | tf_op jit(solution)/shard_map/all_to_all | solution.py:157
  271.6 5.0 %reshape.123 = bf16[2688,1,96]{2,1,0:T(2,128)(2,1)S(1)} reshape(bf16[16,2,8064]{2,1,0:T(2,128)(2,1)} %all-to-all-done.1) | data formatting | bytes 1032192
  276.6 2.8 copy.81
  279.4 3.3 %all_to_all.26 = bf16[1,96,16,168]{3,2,1,0:T(8,128)(2,1)S(1)} reshape(bf16[1,96,2688]{2,1,0:T(8,128)(2,1)} %copy.81) | data formatting | bytes 1032192 | tf_op jit(solution)/shard_map/all_to_all | solution.py:157
  282.7 1.2 copy.82
  283.9 0.7 reshape.116
  284.6 1.2 fusion.23
  (40 shorter events, 0.4 us)
Async XLA Ops:
  7.2 108.9 %copy-start = (bf16[256,2688]{1,0:T(8,128)(2,1)S(1)}, bf16[256,2688]{1,0:T(8,128)(2,1)}, u32[]{:S(2)}) copy-start(bf16[256,2688]{1,0:T(8,128)(2,1)} %param.33) | copy-start | bytes 4128772
  7.2 29.3 %copy-start.5 = (bf16[96,3,128]{2,0,1:T(8,128)(2,1)S(1)}, bf16[96,3,128]{2,0,1:T(8,128)(2,1)}, u32[]{:S(2)}) copy-start(bf16[96,3,128]{2,0,1:T(8,128)(2,1)} %param.26) | copy-start | bytes 221188
  7.2 165.5 %reduce-scatter.4.cloned.1.call-start = ((), (), s32[]{:S(2)}) async-start(), calls=%async_computation.3 | async-start | bytes 1462272
  7.3 47.8 %copy-start.2 = (bf16[2688,2,256]{2,1,0:T(2,128)(2,1)S(1)}, bf16[2688,2,256]{2,1,0:T(2,128)(2,1)}, u32[]{:S(2)}) copy-start(bf16[2688,2,256]{2,1,0:T(2,128)(2,1)} %param.22) | copy-start | bytes 8257540
  55.5 1.3 copy-start.7
  55.6 1.3 copy-start.4
  55.6 1.4 copy-start.10
  55.6 1.4 copy-start.9
  55.6 1.4 copy-start.11
  64.9 4.8 %copy-start.1 = (f32[96,4,64,128]{3,2,1,0:T(8,128)}, f32[96,4,64,128]{3,2,1,0:T(8,128)S(1)}, u32[]{:S(2)}) copy-start(f32[96,4,64,128]{3,2,1,0:T(8,128)S(1)} %multiply_add_fusion) | copy-start | bytes 37748740
  69.7 14.8 %copy-start.8 = (f32[4]{0:T(128)S(1)}, f32[4]{0:T(128)}, u32[]{:S(2)}) copy-start(f32[4]{0:T(128)} %param.31) | copy-start | bytes 52
  69.7 46.4 %copy-start.12 = (bf16[256]{0:T(256)(128)(2,1)S(1)}, bf16[256]{0:T(256)(128)(2,1)}, u32[]{:S(2)}) copy-start(bf16[256]{0:T(256)(128)(2,1)} %param.32) | copy-start | bytes 1540
  84.4 33.6 %copy-start.6 = (s32[96,6]{0,1:T(8,128)S(1)}, s32[96,6]{0,1:T(8,128)}, u32[]{:S(2)}) copy-start(s32[96,6]{0,1:T(8,128)} %param.37) | copy-start | bytes 6916
  84.6 88.1 %copy-start.3 = (bf16[96,168]{0,1:T(8,128)(2,1)S(1)}, bf16[96,168]{0,1:T(8,128)(2,1)}, u32[]{:S(2)}) copy-start(bf16[96,168]{0,1:T(8,128)(2,1)} %param.20) | copy-start | bytes 96772
  253.2 18.4 %all-to-all-start.1 = ((bf16[16,2,8064]{2,1,0:T(2,128)(2,1)}), bf16[16,2,8064]{2,1,0:T(2,128)(2,1)}, u32[]{:S(2)}, u32[]{:S(2)}) async-start(bf16[16,2,8064]{2,1,0:T(2,128)(2,1)} %reshape.122), calls=%async_computation.1 | async-start | bytes 1032192 | tf_op jit(solution)/shard_map/all_to_all | solution.py:157
Sparse Core Ops, SparseCore 0:
  118.0 54.5 reduce-scatter.3
where the time goes:
time: 293 us
  blocking collectives  127 us (43%)
  waiting for transfers between devices  64.1 us (22%)
  other arithmetic  29 us (10%)
  matrix products  29 us (10%)
  local copies, waits for them, and re-layouts  24.6 us (8%)
  between operations  14.5 us (5%)
  starting transfers between devices  4.53 us (2%)
    unnamed x2, waiting for transfers between devices  50.8 us
    psum x1, blocking collectives, local(): group_squares = lax.psum(partial_squares, 'wide')  31.1 us
    psum x1, blocking collectives, local(): lax.psum((jnp.sum(hidden_slice * hidden_slice, axis=1), jnp.dot(weighted,...  30.5 us
    all_gather x1, blocking collectives, local(): full_tokens = lax.all_gather(tokens, 'wide', axis=1, tiled=True)  25.6 us
    all_to_all x1, blocking collectives, local(): lax.all_to_all(sent, 'wide', split_axis=0, concat_axis=2, tiled=True)[0]  21.2 us
    all_gather x1, blocking collectives, local(): all_maps = lax.all_gather(conv_maps, 'wide', axis=1, tiled=True)  18.5 us
    unnamed x1, other arithmetic  14.9 us
    dot_general x1, matrix products, local(): jnp.einsum('shpn,sn->shp', new_state, out_maps, precision=lax.Precision.H...  14.7 us
  transfers between devices with their start and end apart: 2, of which 2 were waited for; matrix products, arithmetic and copies ran while one was open for 2% of the time, Pallas kernels for 0%

commit v1 on v0

v1 whole, which is shorter than its diff:
```python
import functools

import jax
import jax.numpy as jnp
from jax import lax
from jax.experimental import pallas as pl
from jax.experimental.pallas import tpu as pltpu
from jax.sharding import PartitionSpec as P

HEADS = 64
HEAD_DIM = 64
STATE = 128
GROUPS = 8
EPSILON = 1e-05
MESH = pl.DeviceIdType.MESH
F32 = jnp.float32
BF16 = jnp.bfloat16


def greet_all(n, me):
    barrier = pltpu.get_barrier_semaphore()

    def greet(k, carry):
        pl.semaphore_signal(
            barrier, inc=1, device_id={"wide": lax.rem(me + k, n)}, device_id_type=MESH
        )
        return carry

    lax.fori_loop(1, n, greet, 0)


def await_all(n):
    pl.semaphore_wait(pltpu.get_barrier_semaphore(), n - 1)


def exchange_start(n, me, source_of, landing, send_sems, recv_sems):
    def start(k, carry):
        peer = lax.rem(me + k, n)
        pltpu.make_async_remote_copy(
            src_ref=source_of(peer),
            dst_ref=landing.at[me],
            send_sem=send_sems.at[peer],
            recv_sem=recv_sems.at[me],
            device_id={"wide": peer},
            device_id_type=MESH,
        ).start()
        return carry

    lax.fori_loop(1, n, start, 0)


def exchange_wait(n, me, source_of, landing, send_sems, recv_sems):
    def finish(k, carry):
        peer = lax.rem(me + n - k, n)
        copy = pltpu.make_async_remote_copy(
            src_ref=source_of(peer),
            dst_ref=landing.at[peer],
            send_sem=send_sems.at[peer],
            recv_sem=recv_sems.at[peer],
            device_id={"wide": peer},
            device_id_type=MESH,
        )
        copy.wait_recv()
        copy.wait_send()
        return carry

    lax.fori_loop(1, n, finish, 0)


def gather_kernel(
    n,
    local_heads,
    tokens,
    gain,
    weights_hbm,
    window,
    taps,
    normed_out,
    in_out,
    out_out,
    landing,
    full,
    weights,
    mapped,
    arrived,
    weight_sem,
    send_sems,
    recv_sems,
    map_send,
    map_recv,
):
    me = lax.axis_index("wide")
    width = tokens.shape[1]
    cols = window.shape[2]
    load = pltpu.make_async_copy(weights_hbm, weights, weight_sem)
    load.start()
    greet_all(n, me)
    await_all(n)
    exchange_start(n, me, lambda peer: tokens, landing, send_sems, recv_sems)
    landing[me] = tokens[...]
    exchange_wait(n, me, lambda peer: tokens, landing, send_sems, recv_sems)
    for i in range(n):
        full[:, i * width : (i + 1) * width] = landing[i].astype(F32)
    values = full[...]
    mean = jnp.mean(values * values, axis=1, keepdims=True)
    normed = (values * lax.rsqrt(mean + EPSILON) * gain[...].astype(F32)).astype(BF16)
    normed_out[...] = normed
    load.wait()
    raw = jnp.dot(normed, weights[...], preferred_element_type=F32).astype(BF16).astype(F32)
    kernel = taps[...].astype(F32)
    mixed = raw * kernel[3:4]
    for k in range(3):
        mixed = mixed + window[k].astype(F32) * kernel[k : k + 1]
    mapped[...] = (mixed * jax.nn.sigmoid(mixed)).astype(BF16)
    half = n // 2
    per_group = half // GROUPS
    readers = HEADS // GROUPS // local_heads
    kind = me // half
    own_group = lax.rem(me, half) // per_group
    own_slot = kind * per_group + lax.rem(me, per_group)

    def send(r):
        peer = own_group * readers + r
        return peer, pltpu.make_async_remote_copy(
            src_ref=mapped,
            dst_ref=arrived.at[own_slot],
            send_sem=map_send.at[r],
            recv_sem=map_recv.at[own_slot],
            device_id={"wide": peer},
            device_id_type=MESH,
        )

    for r in range(readers):
        peer, copy = send(r)

        @pl.when(peer != me)
        def _():
            copy.start()

        @pl.when(peer == me)
        def _():
            arrived[own_slot] = mapped[...]

    group = me // readers
    for slot in range(2 * per_group):
        origin = (slot // per_group) * half + group * per_group + slot % per_group

        @pl.when(origin != me)
        def _():
            pltpu.make_async_remote_copy(
                src_ref=mapped,
                dst_ref=arrived.at[slot],
                send_sem=map_send.at[0],
                recv_sem=map_recv.at[slot],
                device_id={"wide": me},
                device_id_type=MESH,
            ).wait_recv()

    for slot in range(per_group):
        in_out[:, slot * cols : (slot + 1) * cols] = arrived[slot].astype(F32)
        out_out[:, slot * cols : (slot + 1) * cols] = arrived[per_group + slot].astype(F32)
    for r in range(readers):
        peer, copy = send(r)

        @pl.when(peer != me)
        def _():
            copy.wait_send()


def state_kernel(
    rows, heads, decay, state, driven, inputs, gates, skips, in_maps, out_maps, new_state, gated
):
    base = pl.program_id(0) * rows
    columns = driven[...].T
    readers = out_maps[...].astype(BF16)
    row_ids = lax.broadcasted_iota(jnp.int32, (rows, heads * HEAD_DIM), 0)
    total = jnp.zeros((rows, heads * HEAD_DIM), F32)
    for j in range(rows):
        maps = in_maps[j : j + 1, :]
        parts = []
        for h in range(heads):
            column = columns[h * HEAD_DIM : (h + 1) * HEAD_DIM, j : j + 1]
            fresh = decay[(base + j) * heads + h] * state[j, h] + column * maps
            new_state[j, h] = fresh
            parts.append(fresh.astype(BF16))
        block = jnp.concatenate(parts, axis=0)
        found = lax.dot_general(
            readers, block, (((1,), (1,)), ((), ())), preferred_element_type=F32
        )
        total = jnp.where(row_ids == j, found, total)
    readout = total + skips[...] * inputs[...]
    gate = gates[...].astype(F32)
    gated[...] = readout * (gate * jax.nn.sigmoid(gate))


def expert_kernel(
    n,
    partners,
    gated,
    gated_gain,
    proj_out,
    tokens,
    moe_gain,
    router_hi,
    router_lo,
    expert_ids,
    up_hbm,
    down_hbm,
    result,
    up,
    down,
    terms,
    outgoing,
    landing,
    hidden_own,
    hidden_all,
    returning,
    returned,
    squares,
    squares_in,
    load_sems,
    square_send,
    square_recv,
    mix_send,
    mix_recv,
    hid_send,
    hid_recv,
    ret_send,
    ret_recv,
):
    me = lax.axis_index("wide")
    seqs, width = tokens.shape
    load_up = pltpu.make_async_copy(up_hbm, up, load_sems.at[0])
    load_down = pltpu.make_async_copy(down_hbm, down, load_sems.at[1])
    load_up.start()
    load_down.start()
    greet_all(n, me)
    values = gated[...]
    own_squares = jnp.sum(values * values, axis=1, keepdims=True)
    squares[...] = jnp.broadcast_to(own_squares, squares.shape)
    await_all(n)
    first = (me // partners) * partners
    place = lax.rem(me, partners)

    def partner_copy(k):
        other = lax.rem(place + k, partners)
        return pltpu.make_async_remote_copy(
            src_ref=squares,
            dst_ref=squares_in.at[k - 1],
            send_sem=square_send.at[k - 1],
            recv_sem=square_recv.at[k - 1],
            device_id={"wide": first + other},
            device_id_type=MESH,
        )

    for k in range(1, partners):
        partner_copy(k).start()
    weighted = (values * gated_gain[...].astype(F32)).astype(BF16)
    terms[...] = jnp.dot(weighted, proj_out[...], preferred_element_type=F32)
    total = own_squares
    for k in range(1, partners):
        partner_copy(k).wait()
        total = total + squares_in[k - 1][:, :1]
    channels = values.shape[1] * partners
    scale = lax.rsqrt(total / channels + EPSILON)
    for i in range(n):
        outgoing[i] = (terms[:, i * width : (i + 1) * width] * scale).astype(BF16)
    exchange_start(n, me, lambda peer: outgoing.at[peer], landing, mix_send, mix_recv)
    landing[me] = outgoing[me]
    exchange_wait(n, me, lambda peer: outgoing.at[peer], landing, mix_send, mix_recv)
    hidden = tokens[...].astype(F32)
    mixed = landing[0].astype(F32)
    for i in range(1, n):
        mixed = mixed + landing[i].astype(F32)
    hidden_own[...] = (hidden + mixed).astype(BF16)
    exchange_start(n, me, lambda peer: hidden_own, hidden_all, hid_send, hid_recv)
    hidden_all[me] = hidden_own[...]
    exchange_wait(n, me, lambda peer: hidden_own, hidden_all, hid_send, hid_recv)
    for i in range(n):
        terms[:, i * width : (i + 1) * width] = hidden_all[i].astype(F32)
    values = terms[...]
    mean = jnp.mean(values * values, axis=1, keepdims=True)
    moe_scale = lax.rsqrt(mean + EPSILON)
    rounded = values.astype(BF16)
    logits = moe_scale * (
        jnp.dot(rounded, router_hi[...], preferred_element_type=F32)
        + jnp.dot(rounded, router_lo[...], preferred_element_type=F32)
    )
    expert = lax.broadcasted_iota(jnp.int32, logits.shape, 1)
    named = jnp.zeros(logits.shape, F32)
    for k in range(expert_ids.shape[1]):
        named = named + jnp.where(expert == expert_ids[:, k : k + 1], 1.0, 0.0)
    score = named * jax.nn.sigmoid(logits)
    mine = jnp.sum(jnp.where(expert == me, score, 0.0), axis=1, keepdims=True)
    weight = mine / jnp.sum(score, axis=1, keepdims=True)
    moe_input = (values * moe_scale * moe_gain[...].astype(F32)).astype(BF16)
    load_up.wait()
    units = jnp.dot(moe_input, up[0], preferred_element_type=F32)
    active = jnp.square(jnp.maximum(units, 0.0)).astype(BF16)
    load_down.wait()
    terms[...] = jnp.dot(active, down[0], preferred_element_type=F32)
    for i in range(n):
        served = terms[:, i * width : (i + 1) * width].astype(BF16).astype(F32)
        returning[i] = (served * weight).astype(BF16)
    exchange_start(n, me, lambda peer: returning.at[peer], returned, ret_send, ret_recv)
    returned[me] = returning[me]
    exchange_wait(n, me, lambda peer: returning.at[peer], returned, ret_send, ret_recv)
    mixed = returned[0].astype(F32)
    for i in range(1, n):
        mixed = mixed + returned[i].astype(F32)
    result[...] = (hidden_own[...].astype(F32) + mixed).astype(BF16)


def convolve(window, fresh, kernel):
    stacked = jnp.concatenate([window, fresh[:, None, :]], axis=1).astype(F32)
    return jax.nn.silu(jnp.sum(stacked * kernel.astype(F32)[None], axis=1)).astype(BF16)


def vmem(count):
    return [pl.BlockSpec(memory_space=pltpu.VMEM)] * count


ANY = pl.BlockSpec(memory_space=pl.ANY)
DMA = pltpu.SemaphoreType.DMA


def local(
    n,
    tokens,
    mix_gain,
    proj_inner,
    proj_maps,
    proj_step,
    window_inner,
    window_maps,
    kernel_inner,
    kernel_maps,
    step_bias,
    decay_log,
    skip_gain,
    gated_gain,
    proj_out,
    ssm_state,
    moe_gain,
    router_weight,
    expert_ids,
    expert_up,
    expert_down,
):
    seqs, width = tokens.shape
    full_width = proj_inner.shape[0]
    inner = proj_inner.shape[2]
    cols = proj_maps.shape[1]
    heads = proj_step.shape[1]
    readers = HEADS // GROUPS // heads
    slots = 2 * (STATE // cols)
    normed, in_maps, out_maps = pl.pallas_call(
        functools.partial(gather_kernel, n, heads),
        out_shape=(
            jax.ShapeDtypeStruct((seqs, full_width), BF16),
            jax.ShapeDtypeStruct((seqs, STATE), F32),
            jax.ShapeDtypeStruct((seqs, STATE), F32),
        ),
        in_specs=vmem(2) + [ANY] + vmem(2),
        out_specs=tuple(vmem(3)),
        scratch_shapes=[
            pltpu.VMEM((n, seqs, width), BF16),
            pltpu.VMEM((seqs, full_width), F32),
            pltpu.VMEM((full_width, cols), BF16),
            pltpu.VMEM((seqs, cols), BF16),
            pltpu.VMEM((slots, seqs, cols), BF16),
            DMA(()),
            DMA((n,)),
            DMA((n,)),
            DMA((readers,)),
            DMA((slots,)),
        ],
        compiler_params=pltpu.CompilerParams(collective_id=0, has_side_effects=True),
        name="gather_tokens",
    )(tokens, mix_gain[None], proj_maps, window_maps.transpose(1, 0, 2), kernel_maps)
    both = jnp.dot(
        normed, proj_inner.reshape(full_width, 2 * inner), preferred_element_type=F32
    ).astype(BF16)
    step_raw = jnp.dot(normed, proj_step, preferred_element_type=F32).astype(BF16)
    conv_inner = convolve(window_inner, both[:, inner:], kernel_inner).astype(F32)
    step_size = jax.nn.softplus(step_raw.astype(F32) + step_bias)
    decay = jnp.exp(-jnp.exp(decay_log) * step_size)
    driven = jnp.repeat(step_size, HEAD_DIM, axis=1) * conv_inner
    rows = 8
    skips = jnp.repeat(skip_gain, HEAD_DIM)[None]
    by_row = lambda i: (i, 0)
    by_state = lambda i: (i, 0, 0, 0)
    new_state, gated = pl.pallas_call(
        functools.partial(state_kernel, rows, heads),
        grid=(seqs // rows,),
        out_shape=(
            jax.ShapeDtypeStruct(ssm_state.shape, F32),
            jax.ShapeDtypeStruct((seqs, inner), F32),
        ),
        in_specs=[
            pl.BlockSpec(memory_space=pltpu.SMEM),
            pl.BlockSpec((rows, heads, HEAD_DIM, STATE), by_state),
            pl.BlockSpec((rows, inner), by_row),
            pl.BlockSpec((rows, inner), by_row),
            pl.BlockSpec((rows, inner), by_row),
            pl.BlockSpec((1, inner), lambda i: (0, 0)),
            pl.BlockSpec((rows, STATE), by_row),
            pl.BlockSpec((rows, STATE), by_row),
        ],
        out_specs=(
            pl.BlockSpec((rows, heads, HEAD_DIM, STATE), by_state),
            pl.BlockSpec((rows, inner), by_row),
        ),
        name="update_state",
    )(
        decay.reshape(-1),
        ssm_state,
        driven,
        conv_inner,
        both[:, :inner].astype(F32),
        skips,
        in_maps,
        out_maps,
    )
    folded = router_weight.astype(F32) * moe_gain.astype(F32)[:, None]
    router_hi = folded.astype(BF16)
    router_lo = (folded - lax.optimization_barrier(router_hi).astype(F32)).astype(BF16)
    piece = pltpu.VMEM((n, seqs, width), BF16)
    next_hidden = pl.pallas_call(
        functools.partial(expert_kernel, n, readers),
        out_shape=jax.ShapeDtypeStruct((seqs, width), BF16),
        in_specs=vmem(8) + [ANY, ANY],
        out_specs=vmem(1)[0],
        scratch_shapes=[
            pltpu.VMEM(expert_up.shape, BF16),
            pltpu.VMEM(expert_down.shape, BF16),
            pltpu.VMEM((seqs, full_width), F32),
            piece,
            piece,
            pltpu.VMEM((seqs, width), BF16),
            piece,
            piece,
            piece,
            pltpu.VMEM((seqs, 128), F32),
            pltpu.VMEM((readers - 1, seqs, 128), F32),
            DMA((2,)),
            DMA((readers - 1,)),
            DMA((readers - 1,)),
        ]
        + [DMA((n,))] * 6,
        compiler_params=pltpu.CompilerParams(collective_id=1, has_side_effects=True),
        name="mix_and_serve",
    )(
        gated,
        gated_gain[None],
        proj_out,
        tokens,
        moe_gain[None],
        router_hi,
        router_lo,
        expert_ids,
        expert_up,
        expert_down,
    )
    return (next_hidden, new_state)


def solution(mesh):
    in_specs = (
        P("group", "wide"),
        P(),
        P(None, None, "wide"),
        P(None, "wide"),
        P(None, "wide"),
        P("group", None, "wide"),
        P("group", None, "wide"),
        P(None, "wide"),
        P(None, "wide"),
        P("wide"),
        P("wide"),
        P("wide"),
        P("wide"),
        P("wide", None),
        P("group", "wide", None, None),
        P(),
        P(),
        P("group", None),
        P("wide", None, None),
        P("wide", None, None),
    )
    out_specs = (P("group", "wide"), P("group", "wide", None, None))
    body = functools.partial(local, mesh.shape["wide"])
    return jax.shard_map(body, mesh=mesh, in_specs=in_specs, out_specs=out_specs, check_vma=False)
```

time: 293 us -> 131 us (0.45)
  the two profiles are of different devices: /device:TPU:0 before, /device:TPU:29 now
where the time goes in v1:
time: 131 us; the launch traced here: 130 us
  Pallas kernels  107 us (82%)
  local copies, waits for them, and re-layouts  18.3 us (14%)
  other arithmetic  3.1 us (2%)
    pallas_call x1, Pallas kernels, local(): pl.pallas_call(functools.partial(expert_kernel, n, readers), out_shape=ja...  65.2 us
    pallas_call x1, Pallas kernels, local(): pl.pallas_call(functools.partial(gather_kernel, n, heads), out_shape=(jax...  26.7 us
    pallas_call x1, Pallas kernels, local(): pl.pallas_call(functools.partial(state_kernel, rows, heads), grid=(seqs /...  15.1 us
    unnamed x29, local copies, waits for them, and re-layouts  14 us

profile of v1, /device:TPU:29, one launch (start us, length us, event | category | flops | bytes accessed | tf_op | source)
XLA Modules:
  0.0 130.1 jit_solution(7757570627266521889)
XLA Ops:
  0.6 0.0 copy-start
  0.6 1.5 %copy.37.tokens = bf16[96,168]{1,0:T(8,128)(2,1)} copy(bf16[96,168]{0,1:T(8,128)(2,1)} %param.20) | data formatting | bytes 64512 | tf_op args[0]
  2.1 1.3 broadcast_in_dim.22.gain
  3.4 26.7 %gather_tokens.1 = (bf16[96,2688]{1,0:T(8,128)(2,1)}, f32[96,128]{1,0:T(8,128)}, f32[96,128]{1,0:T(8,128)}) custom-call(bf16[96,168]{1,0:T(8,128)(2,1)} %copy.37.tokens, bf16[1,2688]{1,0:T(2,128)(2,1)} %broadcast_in_dim.22.gain, bf16[2688,128]{1,0:T(8,128)(2,1)} %weights_hbm.1, bf16[3,96,128]{2,1,0:T(8,128)(2,1)} %bitcast.13, bf16[4,128]{1,0:T(4,128)(2,1)} %taps.1), custom_call_target="tpu_custom_call" | custom-call | tf_op jit(solution)/shard_map/gather_tokens/pallas_call | solution.py:357
  30.1 0.0 copy-start.2
  30.2 2.3 %copy.46 = bf16[336,8,2,256]{3,1,2,0:T(8,128)(2,1)S(1)} copy(bf16[336,8,2,256]{3,2,1,0:T(2,128)(2,1)} %bitcast.11) | data formatting | bytes 5505024
  32.5 0.0 copy-start.7
  32.5 0.0 copy-start.3
  32.5 0.0 copy-start.9
  32.5 0.0 copy-start.10
  32.5 0.0 copy-start.8
  32.5 0.0 copy-done.2
  32.5 0.6 convolution_convert_fusion
  33.1 0.6 slice_convert_fusion
  33.8 0.0 copy-done.7
  33.8 0.0 copy-done.3
  33.8 0.0 copy-done.9
  33.8 0.0 copy-done
  33.8 0.0 copy-done.10
  33.9 0.3 multiply_exponential_fusion
  34.2 0.1 copy.39
  34.3 0.7 fusion.2
  35.0 0.1 copy.38
  35.1 0.7 reshape.17.decay
  35.8 0.0 copy-done.8
  35.8 0.1 broadcast_in_dim.25
  35.8 0.6 broadcast_in_dim_reshape.3.skips
  36.5 0.0 copy-start.4
  36.5 0.0 copy-start.5
  36.5 15.1 %update_state.1 = (f32[96,4,64,128]{3,2,1,0:T(8,128)}, f32[96,256]{1,0:T(8,128)}) custom-call(f32[384]{0:T(512)} %reshape.17.decay, f32[96,4,64,128]{3,2,1,0:T(8,128)} %state.1, f32[96,256]{1,0:T(8,128)} %get-tuple-element.21.driven, f32[96,256]{1,0:T(8,128)} %get-tuple-element.20.inputs, f32[96,256]{1,0:T(8,128)} %get-tuple-element.18.gates, ...), custom_call_target="tpu_custom_call" | custom-call | tf_op jit(solution)/shard_map/update_state/pallas_call | solution.py:393
  51.6 0.0 copy-done.4
  51.6 0.3 copy.40
  51.9 0.0 copy-done.5
  51.9 0.4 multiply_convert_fusion.router_hi
  52.3 0.0 copy-start.1
  52.4 1.3 subtract_convert_fusion.router_lo
  53.6 0.0 copy-start.6
  53.6 0.0 copy-start.11
  53.6 7.9 %copy.44.up_hbm = bf16[1,2688,928]{2,1,0:T(8,128)(2,1)} copy(bf16[1,2688,928]{1,2,0:T(8,128)(2,1)} %param.38) | data formatting | bytes 9977856 | tf_op args[18]
  61.5 0.0 copy-done.1
  61.5 0.0 copy-done.6
  61.5 0.7 copy.43.expert_ids
  62.2 0.6 broadcast_in_dim.27.moe_gain
  62.8 0.0 copy-done.11
  62.8 0.6 broadcast_in_dim.26.gated_gain
  63.4 65.2 %mix_and_serve.1 = bf16[96,168]{1,0:T(8,128)(2,1)} custom-call(f32[96,256]{1,0:T(8,128)} %get-tuple-element.10.gated, bf16[1,256]{1,0:T(2,128)(2,1)} %broadcast_in_dim.26.gated_gain, bf16[256,2688]{1,0:T(8,128)(2,1)} %proj_out.1, bf16[96,168]{1,0:T(8,128)(2,1)} %copy.37.tokens, bf16[1,2688]{1,0:T(2,128)(2,1)} %broadcast_in_dim.27.moe_gain, ...), custom_call_target="tpu_custom_call" | custom-call | tf_op jit(solution)/shard_map/mix_and_serve/pallas_call | solution.py:429
  128.6 1.5 %copy.45 = bf16[96,168]{0,1:T(8,128)(2,1)} copy(bf16[96,168]{1,0:T(8,128)(2,1)} %mix_and_serve.1) | data formatting | bytes 64512
  (5 shorter events, 0.1 us)
Async XLA Ops:
  0.6 33.2 %copy-start = (bf16[2688,4]{0,1:T(4,128)(2,1)S(1)}, bf16[2688,4]{0,1:T(4,128)(2,1)}, u32[]{:S(2)}) copy-start(bf16[2688,4]{0,1:T(4,128)(2,1)} %param.24) | copy-start | bytes 64516
  30.1 2.4 %copy-start.2 = (bf16[96,2688]{1,0:T(8,128)(2,1)S(1)}, bf16[96,2688]{1,0:T(8,128)(2,1)}, u32[]{:S(2)}) copy-start(bf16[96,2688]{1,0:T(8,128)(2,1)} %get-tuple-element.7) | copy-start | bytes 1548292
  32.5 1.3 %copy-start.7 = (bf16[4,256]{1,0:T(4,128)(2,1)S(1)}, bf16[4,256]{1,0:T(4,128)(2,1)}, u32[]{:S(2)}) copy-start(bf16[4,256]{1,0:T(4,128)(2,1)} %param.27) | copy-start | bytes 6148
  32.5 1.3 copy-start.3
  32.5 1.3 %copy-start.9 = (f32[4]{0:T(128)S(1)}, f32[4]{0:T(128)}, u32[]{:S(2)}) copy-start(f32[4]{0:T(128)} %param.30) | copy-start | bytes 52
  32.5 1.4 %copy-start.10 = (f32[4]{0:T(128)S(1)}, f32[4]{0:T(128)}, u32[]{:S(2)}) copy-start(f32[4]{0:T(128)} %param.29) | copy-start | bytes 52
  32.5 3.3 %copy-start.8 = (f32[4]{0:T(128)S(1)}, f32[4]{0:T(128)}, u32[]{:S(2)}) copy-start(f32[4]{0:T(128)} %param.31) | copy-start | bytes 52
  36.5 15.1 %copy-start.4 = (bf16[2688,16]{0,1:T(8,128)(2,1)S(1)}, bf16[2688,16]{0,1:T(8,128)(2,1)}, u32[]{:S(2)}) copy-start(bf16[2688,16]{0,1:T(8,128)(2,1)} %param.36) | copy-start | bytes 258052
  36.5 15.4 %copy-start.5 = (bf16[2688]{0:T(1024)(128)(2,1)S(1)}, bf16[2688]{0:T(1024)(128)(2,1)}, u32[]{:S(2)}) copy-start(bf16[2688]{0:T(1024)(128)(2,1)} %param.35) | copy-start | bytes 16132
  52.3 9.2 %copy-start.1 = (bf16[2688,16]{1,0:T(8,128)(2,1)}, bf16[2688,16]{1,0:T(8,128)(2,1)S(1)}, u32[]{:S(2)}) copy-start(bf16[2688,16]{1,0:T(8,128)(2,1)S(1)} %multiply_convert_fusion.router_hi) | copy-start | bytes 258052
  53.6 7.9 %copy-start.6 = (s32[96,6]{0,1:T(8,128)S(1)}, s32[96,6]{0,1:T(8,128)}, u32[]{:S(2)}) copy-start(s32[96,6]{0,1:T(8,128)} %param.37) | copy-start | bytes 6916
  53.6 9.2 %copy-start.11 = (bf16[256]{0:T(256)(128)(2,1)S(1)}, bf16[256]{0:T(256)(128)(2,1)}, u32[]{:S(2)}) copy-start(bf16[256]{0:T(256)(128)(2,1)} %param.32) | copy-start | bytes 1540

commit v2 on v1

--- a/solution.py
+++ b/solution.py
@@ -33,38 +33,144 @@
     pl.semaphore_wait(pltpu.get_barrier_semaphore(), n - 1)
 
 
-def exchange_start(n, me, source_of, landing, send_sems, recv_sems):
-    def start(k, carry):
-        peer = lax.rem(me + k, n)
-        pltpu.make_async_remote_copy(
-            src_ref=source_of(peer),
-            dst_ref=landing.at[me],
-            send_sem=send_sems.at[peer],
-            recv_sem=recv_sems.at[me],
-            device_id={"wide": peer},
-            device_id_type=MESH,
-        ).start()
-        return carry
-
-    lax.fori_loop(1, n, start, 0)
-
-
-def exchange_wait(n, me, source_of, landing, send_sems, recv_sems):
-    def finish(k, carry):
-        peer = lax.rem(me + n - k, n)
+def place_of(n, me):
+    lines = n // 4
+    return lines, me // 4, lax.rem(me // 2, 2), lax.rem(me, 2)
+
+
+def index_of(line, side, core):
+    return line * 4 + side * 2 + core
+
+
+def gather_all(n, me, own, landing, send_sems, recv_sems, meanwhile=None):
+    lines, line, side, core = place_of(n, me)
+    across = index_of(line, 1 - side, core)
+    partner = index_of(line, side, 1 - core)
+    sent = []
+
+    def send(src, origin, peer):
         copy = pltpu.make_async_remote_copy(
-            src_ref=source_of(peer),
-            dst_ref=landing.at[peer],
-            send_sem=send_sems.at[peer],
-            recv_sem=recv_sems.at[peer],
+            src_ref=src,
+            dst_ref=landing.at[origin],
+            send_sem=send_sems.at[len(sent)],
+            recv_sem=recv_sems.at[origin],
             device_id={"wide": peer},
             device_id_type=MESH,
         )
-        copy.wait_recv()
+        copy.start()
+        sent.append(copy)
+
+    def arrive(origin):
+        pltpu.make_async_remote_copy(
+            src_ref=own,
+            dst_ref=landing.at[origin],
+            send_sem=send_sems.at[0],
+            recv_sem=recv_sems.at[origin],
+            device_id={"wide": partner},
+            device_id_type=MESH,
+        ).wait_recv()
+
+    for k in range(1, lines):
+        send(own, me, index_of(lax.rem(line + k, lines), side, core))
+    send(own, me, across)
+    send(own, me, partner)
+    landing[me] = own[...]
+    if meanwhile is not None:
+        meanwhile()
+    for k in range(1, lines):
+        origin = index_of(lax.rem(line + lines - k, lines), side, core)
+        arrive(origin)
+        send(landing.at[origin], origin, across)
+        send(landing.at[origin], origin, partner)
+    for k in range(lines):
+        origin = index_of(lax.rem(line + lines - k, lines), 1 - side, core)
+        arrive(origin)
+        send(landing.at[origin], origin, partner)
+    for k in range(lines):
+        for other in range(2):
+            arrive(index_of(lax.rem(line + lines - k, lines), other, 1 - core))
+    for copy in sent:
         copy.wait_send()
-        return carry
-
-    lax.fori_loop(1, n, finish, 0)
+
+
+def reduce_all(n, me, blocks, bufs, meanwhile=None):
+    core_in, side_out, side_in, line_out, line_in, sends, core_sem, side_sem, line_sem = bufs
+    lines, line, side, core = place_of(n, me)
+    across = index_of(line, 1 - side, core)
+    partner = index_of(line, side, 1 - core)
+    sent = []
+
+    def copy_of(src, dst, sem, peer, number):
+        return pltpu.make_async_remote_copy(
+            src_ref=src,
+            dst_ref=dst,
+            send_sem=sends.at[number],
+            recv_sem=sem,
+            device_id={"wide": peer},
+            device_id_type=MESH,
+        )
+
+    def send(src, dst, sem, peer):
+        copy = copy_of(src, dst, sem, peer, len(sent))
+        copy.start()
+        sent.append(copy)
+
+    def arrive(dst, sem):
+        copy_of(dst, dst, sem, partner, 0).wait_recv()
+
+    def ahead(k):
+        return lax.rem(line + k, lines)
+
+    for k in range(1, lines + 1):
+        for turn in range(2):
+            other = 1 - side if turn == 0 else side
+            slot = ahead(k) * 2 + other
+            send(
+                blocks.at[index_of(ahead(k), other, 1 - core)],
+                core_in.at[slot],
+                core_sem.at[slot],
+                partner,
+            )
+
+    def pair_sum(k, other):
+        slot = ahead(k) * 2 + other
+        arrive(core_in.at[slot], core_sem.at[slot])
+        return blocks[index_of(ahead(k), other, core)].astype(F32) + core_in[slot].astype(F32)
+
+    def second(k):
+        slot = ahead(k)
+        side_out[slot] = pair_sum(k, 1 - side).astype(BF16)
+        send(side_out.at[slot], side_in.at[slot], side_sem.at[slot], across)
+
+    def third(k):
+        slot = ahead(k)
+        value = pair_sum(k, side)
+        arrive(side_in.at[slot], side_sem.at[slot])
+        value = value + side_in[slot].astype(F32)
+        if k == lines:
+            return value
+        line_out[slot] = value.astype(BF16)
+        send(
+            line_out.at[slot],
+            line_in.at[line],
+            line_sem.at[line],
+            index_of(slot, side, core),
+        )
+
+    second(1)
+    for k in range(1, lines):
+        second(k + 1)
+        third(k)
+    if meanwhile is not None:
+        meanwhile()
+    total = third(lines)
+    for k in range(1, lines):
+        slot = lax.rem(line + lines - k, lines)
+        arrive(line_in.at[slot], line_sem.at[slot])
+        total = total + line_in[slot].astype(F32)
+    for copy in sent:
+        copy.wait_send()
+    return total
 
 
 def gather_kernel(
@@ -90,20 +196,19 @@
     map_recv,
 ):
     me = lax.axis_index("wide")
-    width = tokens.shape[1]
+    width = tokens.shape[0]
     cols = window.shape[2]
     load = pltpu.make_async_copy(weights_hbm, weights, weight_sem)
     load.start()
     greet_all(n, me)
     await_all(n)
-    exchange_start(n, me, lambda peer: tokens, landing, send_sems, recv_sems)
-    landing[me] = tokens[...]
-    exchange_wait(n, me, lambda peer: tokens, landing, send_sems, recv_sems)
+    gather_all(n, me, tokens, landing, send_sems, recv_sems)
     for i in range(n):
-        full[:, i * width : (i + 1) * width] = landing[i].astype(F32)
+        full[i * width : (i + 1) * width, :] = landing[i].astype(F32)
     values = full[...]
-    mean = jnp.mean(values * values, axis=1, keepdims=True)
-    normed = (values * lax.rsqrt(mean + EPSILON) * gain[...].astype(F32)).astype(BF16)
+    mean = jnp.mean(values * values, axis=0, keepdims=True)
+    scaled = (values * lax.rsqrt(mean + EPSILON)).T
+    normed = (scaled * gain[...].astype(F32)).astype(BF16)
     normed_out[...] = normed
     load.wait()
     raw = jnp.dot(normed, weights[...], preferred_element_type=F32).astype(BF16).astype(F32)
@@ -201,8 +306,7 @@
     proj_out,
     tokens,
     moe_gain,
-    router_hi,
-    router_lo,
+    router,
     expert_ids,
     up_hbm,
     down_hbm,
@@ -210,26 +314,23 @@
     up,
     down,
     terms,
+    gains,
+    router_hi,
+    router_lo,
     outgoing,
-    landing,
     hidden_own,
     hidden_all,
-    returning,
-    returned,
     squares,
     squares_in,
     load_sems,
     square_send,
     square_recv,
-    mix_send,
-    mix_recv,
     hid_send,
     hid_recv,
-    ret_send,
-    ret_recv,
+    *bufs,
 ):
     me = lax.axis_index("wide")
-    seqs, width = tokens.shape
+    width, seqs = tokens.shape
     load_up = pltpu.make_async_copy(up_hbm, up, load_sems.at[0])
     load_down = pltpu.make_async_copy(down_hbm, down, load_sems.at[1])
     load_up.start()
@@ -256,59 +357,57 @@
     for k in range(1, partners):
         partner_copy(k).start()
     weighted = (values * gated_gain[...].astype(F32)).astype(BF16)
-    terms[...] = jnp.dot(weighted, proj_out[...], preferred_element_type=F32)
+    mixed = jnp.dot(weighted, proj_out[...], preferred_element_type=F32)
     total = own_squares
     for k in range(1, partners):
         partner_copy(k).wait()
         total = total + squares_in[k - 1][:, :1]
     channels = values.shape[1] * partners
-    scale = lax.rsqrt(total / channels + EPSILON)
+    terms[...] = (mixed * lax.rsqrt(total / channels + EPSILON)).T
     for i in range(n):
-        outgoing[i] = (terms[:, i * width : (i + 1) * width] * scale).astype(BF16)
-    exchange_start(n, me, lambda peer: outgoing.at[peer], landing, mix_send, mix_recv)
-    landing[me] = outgoing[me]
-    exchange_wait(n, me, lambda peer: outgoing.at[peer], landing, mix_send, mix_recv)
-    hidden = tokens[...].astype(F32)
-    mixed = landing[0].astype(F32)
-    for i in range(1, n):
-        mixed = mixed + landing[i].astype(F32)
-    hidden_own[...] = (hidden + mixed).astype(BF16)
-    exchange_start(n, me, lambda peer: hidden_own, hidden_all, hid_send, hid_recv)
-    hidden_all[me] = hidden_own[...]
-    exchange_wait(n, me, lambda peer: hidden_own, hidden_all, hid_send, hid_recv)
+        outgoing[i] = terms[i * width : (i + 1) * width, :].astype(BF16)
+
+    def prepare():
+        gain = moe_gain[...].astype(F32)
+        gains[...] = jnp.broadcast_to(gain, (seqs, gain.shape[1])).T
+        folded = router[...].astype(F32) * gain
+        high = folded.astype(BF16)
+        router_hi[...] = high
+        router_lo[...] = (folded - high.astype(F32)).astype(BF16)
+
+    half = len(bufs) // 2
+    reduced = reduce_all(n, me, outgoing, bufs[:half], prepare)
+    hidden_own[...] = (tokens[...].astype(F32) + reduced).astype(BF16)
+    gather_all(n, me, hidden_own, hidden_all, hid_send, hid_recv)
     for i in range(n):
-        terms[:, i * width : (i + 1) * width] = hidden_all[i].astype(F32)
+        terms[i * width : (i + 1) * width, :] = hidden_all[i].astype(F32)
     values = terms[...]
-    mean = jnp.mean(values * values, axis=1, keepdims=True)
+    mean = jnp.mean(values * values, axis=0, keepdims=True)
     moe_scale = lax.rsqrt(mean + EPSILON)
     rounded = values.astype(BF16)
+    moe_input = (values * moe_scale * gains[...]).astype(BF16)
+    load_up.wait()
+    units = jnp.dot(up[0], moe_input, preferred_element_type=F32)
     logits = moe_scale * (
-        jnp.dot(rounded, router_hi[...], preferred_element_type=F32)
-        + jnp.dot(rounded, router_lo[...], preferred_element_type=F32)
+        jnp.dot(router_hi[...], rounded, preferred_element_type=F32)
+        + jnp.dot(router_lo[...], rounded, preferred_element_type=F32)
     )
-    expert = lax.broadcasted_iota(jnp.int32, logits.shape, 1)
+    expert = lax.broadcasted_iota(jnp.int32, logits.shape, 0)
     named = jnp.zeros(logits.shape, F32)
-    for k in range(expert_ids.shape[1]):
-        named = named + jnp.where(expert == expert_ids[:, k : k + 1], 1.0, 0.0)
+    for k in range(expert_ids.shape[0]):
+        named = named + jnp.where(expert == expert_ids[k : k + 1, :], 1.0, 0.0)
     score = named * jax.nn.sigmoid(logits)
-    mine = jnp.sum(jnp.where(expert == me, score, 0.0), axis=1, keepdims=True)
-    weight = mine / jnp.sum(score, axis=1, keepdims=True)
-    moe_input = (values * moe_scale * moe_gain[...].astype(F32)).astype(BF16)
-    load_up.wait()
-    units = jnp.dot(moe_input, up[0], preferred_element_type=F32)
-    active = jnp.square(jnp.maximum(units, 0.0)).astype(BF16)
+    mine = jnp.sum(jnp.where(expert == me, score, 0.0), axis=0, keepdims=True)
+    weight = mine / jnp.sum(score, axis=0, keepdims=True)
+    active = jnp.square(jnp.maximum(units, 0.0)).T.astype(BF16)
     load_down.wait()
-    terms[...] = jnp.dot(active, down[0], preferred_element_type=F32)
+    served = jnp.dot(active, down[0], preferred_element_type=F32)
+    terms[...] = served.T
     for i in range(n):
-        served = terms[:, i * width : (i + 1) * width].astype(BF16).astype(F32)
-        returning[i] = (served * weight).astype(BF16)
-    exchange_start(n, me, lambda peer: returning.at[peer], returned, ret_send, ret_recv)
-    returned[me] = returning[me]
-    exchange_wait(n, me, lambda peer: returning.at[peer], returned, ret_send, ret_recv)
-    mixed = returned[0].astype(F32)
-    for i in range(1, n):
-        mixed = mixed + returned[i].astype(F32)
-    result[...] = (hidden_own[...].astype(F32) + mixed).astype(BF16)
+        block = terms[i * width : (i + 1) * width, :].astype(BF16).astype(F32)
+        outgoing[i] = (block * weight).astype(BF16)
+    reduced = reduce_all(n, me, outgoing, bufs[half:])
+    result[...] = (hidden_own[...].astype(F32) + reduced).astype(BF16)
 
 
 def convolve(window, fresh, kernel):
@@ -364,8 +463,8 @@
         in_specs=vmem(2) + [ANY] + vmem(2),
         out_specs=tuple(vmem(3)),
         scratch_shapes=[
-            pltpu.VMEM((n, seqs, width), BF16),
-            pltpu.VMEM((seqs, full_width), F32),
+            pltpu.VMEM((n, width, seqs), BF16),
+            pltpu.VMEM((full_width, seqs), F32),
             pltpu.VMEM((full_width, cols), BF16),
             pltpu.VMEM((seqs, cols), BF16),
             pltpu.VMEM((slots, seqs, cols), BF16),
@@ -377,7 +476,7 @@
         ],
         compiler_params=pltpu.CompilerParams(collective_id=0, has_side_effects=True),
         name="gather_tokens",
-    )(tokens, mix_gain[None], proj_maps, window_maps.transpose(1, 0, 2), kernel_maps)
+    )(tokens.T, mix_gain[None], proj_maps, window_maps.transpose(1, 0, 2), kernel_maps)
     both = jnp.dot(
         normed, proj_inner.reshape(full_width, 2 * inner), preferred_element_type=F32
     ).astype(BF16)
@@ -422,47 +521,61 @@
         in_maps,
         out_maps,
     )
-    folded = router_weight.astype(F32) * moe_gain.astype(F32)[:, None]
-    router_hi = folded.astype(BF16)
-    router_lo = (folded - lax.optimization_barrier(router_hi).astype(F32)).astype(BF16)
-    piece = pltpu.VMEM((n, seqs, width), BF16)
+    lines = n // 4
+
+    def piece(count):
+        return pltpu.VMEM((count, width, seqs), BF16)
+
+    reduce_bufs = [
+        piece(2 * lines),
+        piece(lines),
+        piece(lines),
+        piece(lines),
+        piece(lines),
+        DMA((4 * lines - 1,)),
+        DMA((2 * lines,)),
+        DMA((lines,)),
+        DMA((lines,)),
+    ]
+    up_shape = (1, expert_up.shape[2], full_width)
     next_hidden = pl.pallas_call(
         functools.partial(expert_kernel, n, readers),
-        out_shape=jax.ShapeDtypeStruct((seqs, width), BF16),
-        in_specs=vmem(8) + [ANY, ANY],
+        out_shape=jax.ShapeDtypeStruct((width, seqs), BF16),
+        in_specs=vmem(7) + [ANY, ANY],
         out_specs=vmem(1)[0],
         scratch_shapes=[
-            pltpu.VMEM(expert_up.shape, BF16),
+            pltpu.VMEM(up_shape, BF16),
             pltpu.VMEM(expert_down.shape, BF16),
-            pltpu.VMEM((seqs, full_width), F32),
-            piece,
-            piece,
-            pltpu.VMEM((seqs, width), BF16),
-            piece,
-            piece,
-            piece,
+            pltpu.VMEM((full_width, seqs), F32),
+            pltpu.VMEM((full_width, seqs), F32),
+            pltpu.VMEM((router_weight.shape[1], full_width), BF16),
+            pltpu.VMEM((router_weight.shape[1], full_width), BF16),
+            piece(n),
+            pltpu.VMEM((width, seqs), BF16),
+            piece(n),
             pltpu.VMEM((seqs, 128), F32),
             pltpu.VMEM((readers - 1, seqs, 128), F32),
             DMA((2,)),
             DMA((readers - 1,)),
             DMA((readers - 1,)),
+            DMA((n,)),
+            DMA((n,)),
         ]
-        + [DMA((n,))] * 6,
+        + reduce_bufs * 2,
         compiler_params=pltpu.CompilerParams(collective_id=1, has_side_effects=True),
         name="mix_and_serve",
     )(
         gated,
         gated_gain[None],
         proj_out,
-        tokens,
+        tokens.T,
         moe_gain[None],
-        router_hi,
-        router_lo,
-        expert_ids,
-        expert_up,
+        router_weight.T,
+        expert_ids.T,
+        expert_up.swapaxes(1, 2),
         expert_down,
     )
-    return (next_hidden, new_state)
+    return (next_hidden.T, new_state)
 
 
 def solution(mesh):

time: 131 us -> 91.8 us (0.70)
  the two profiles are of different devices: /device:TPU:29 before, /device:TPU:0 now
where the time goes in v2:
time: 91.8 us; the launch traced here: 91.1 us
  Pallas kernels  80.2 us (87%)
  local copies, waits for them, and re-layouts  7.89 us (9%)
  other arithmetic  1.41 us (2%)
    pallas_call x1, Pallas kernels, local(): pl.pallas_call(functools.partial(expert_kernel, n, readers), out_shape=ja...  43.6 us
    pallas_call x1, Pallas kernels, local(): pl.pallas_call(functools.partial(gather_kernel, n, heads), out_shape=(jax...  21.4 us
    pallas_call x1, Pallas kernels, local(): pl.pallas_call(functools.partial(state_kernel, rows, heads), grid=(seqs /...  15.2 us
    unnamed x20, local copies, waits for them, and re-layouts  3.75 us

profile of v2, /device:TPU:0, one launch (start us, length us, event | category | flops | bytes accessed | tf_op | source)
XLA Modules:
  0.0 91.1 jit_solution(752231199211835216)
XLA Ops:
  0.6 0.0 copy-start
  0.6 1.3 %broadcast_in_dim.21.gain = bf16[1,2688]{1,0:T(2,128)(2,1)} reshape(bf16[2688]{0:T(1024)(128)(2,1)} %param.21) | data formatting | bytes 10752 | tf_op jit(solution)/shard_map/broadcast_in_dim | solution.py:479
  1.9 21.4 %gather_tokens.1 = (bf16[96,2688]{1,0:T(8,128)(2,1)}, f32[96,128]{1,0:T(8,128)}, f32[96,128]{1,0:T(8,128)}) custom-call(bf16[168,96]{1,0:T(8,128)(2,1)} %bitcast.20, bf16[1,2688]{1,0:T(2,128)(2,1)} %broadcast_in_dim.21.gain, bf16[2688,128]{1,0:T(8,128)(2,1)} %weights_hbm.1, bf16[3,96,128]{2,1,0:T(8,128)(2,1)} %bitcast.23, bf16[4,128]{1,0:T(4,128)(2,1)} %taps.1), custom_call_target="tpu_custom_call" | custom-call | tf_op jit(solution)/shard_map/gather_tokens/pallas_call | solution.py:456
  23.4 0.0 copy-start.1
  23.4 2.3 %copy.25 = bf16[336,8,2,256]{3,1,2,0:T(8,128)(2,1)S(1)} copy(bf16[336,8,2,256]{3,2,1,0:T(2,128)(2,1)} %bitcast.17) | data formatting | bytes 5505024
  25.7 0.0 copy-start.4
  25.7 0.0 copy-start.2
  25.7 0.0 copy-start.6
  25.7 0.0 copy-start.7
  25.7 0.0 copy-start.5
  25.7 0.0 copy-done.1
  25.8 0.6 convolution_convert_fusion
  26.3 0.7 slice_convert_fusion
  27.0 0.0 copy-done.4
  27.0 0.0 copy-done.2
  27.1 0.0 copy-done.6
  27.1 0.0 copy-done
  27.1 0.0 copy-done.7
  27.1 0.3 multiply_exponential_fusion
  27.4 0.1 copy.24
  27.5 0.7 fusion.2
  28.2 0.1 copy.23
  28.3 0.7 reshape.16.decay
  29.0 0.0 copy-done.5
  29.0 0.1 broadcast_in_dim.24
  29.1 0.7 broadcast_in_dim_reshape.3.skips
  29.7 0.0 copy-start.3
  29.7 0.0 copy-start.8
  29.7 15.2 %update_state.1 = (f32[96,4,64,128]{3,2,1,0:T(8,128)}, f32[96,256]{1,0:T(8,128)}) custom-call(f32[384]{0:T(512)} %reshape.16.decay, f32[96,4,64,128]{3,2,1,0:T(8,128)} %state.1, f32[96,256]{1,0:T(8,128)} %get-tuple-element.15.driven, f32[96,256]{1,0:T(8,128)} %get-tuple-element.14.inputs, f32[96,256]{1,0:T(8,128)} %get-tuple-element.12.gates, ...), custom_call_target="tpu_custom_call" | custom-call | tf_op jit(solution)/shard_map/update_state/pallas_call | solution.py:492
  44.9 0.0 copy-done.3
  44.9 0.6 broadcast_in_dim.26.moe_gain
  45.5 0.0 copy-done.8
  45.5 0.6 broadcast_in_dim.25.gated_gain
  46.1 43.6 %mix_and_serve.1 = bf16[168,96]{1,0:T(8,128)(2,1)} custom-call(f32[96,256]{1,0:T(8,128)} %get-tuple-element.10.gated, bf16[1,256]{1,0:T(2,128)(2,1)} %broadcast_in_dim.25.gated_gain, bf16[256,2688]{1,0:T(8,128)(2,1)} %proj_out.1, bf16[168,96]{1,0:T(8,128)(2,1)} %bitcast.21, bf16[1,2688]{1,0:T(2,128)(2,1)} %broadcast_in_dim.26.moe_gain, ...), custom_call_target="tpu_custom_call" | custom-call | tf_op jit(solution)/shard_map/mix_and_serve/pallas_call | solution.py:541
  89.7 1.4 %copy.27 = bf16[96,168]{0,1:T(8,128)(2,1)} copy(bf16[96,168]{0,1:T(8,128)(2,1)} %bitcast.19) | data formatting | bytes 64512
  (4 shorter events, 0.1 us)
Async XLA Ops:
  0.6 26.5 %copy-start = (bf16[2688,4]{0,1:T(4,128)(2,1)S(1)}, bf16[2688,4]{0,1:T(4,128)(2,1)}, u32[]{:S(2)}) copy-start(bf16[2688,4]{0,1:T(4,128)(2,1)} %param.24) | copy-start | bytes 64516
  23.4 2.4 %copy-start.1 = (bf16[96,2688]{1,0:T(8,128)(2,1)S(1)}, bf16[96,2688]{1,0:T(8,128)(2,1)}, u32[]{:S(2)}) copy-start(bf16[96,2688]{1,0:T(8,128)(2,1)} %get-tuple-element.7) | copy-start | bytes 1548292
  25.7 1.3 %copy-start.4 = (bf16[4,256]{1,0:T(4,128)(2,1)S(1)}, bf16[4,256]{1,0:T(4,128)(2,1)}, u32[]{:S(2)}) copy-start(bf16[4,256]{1,0:T(4,128)(2,1)} %param.27) | copy-start | bytes 6148
  25.7 1.3 %copy-start.2 = (bf16[96,3,256]{2,0,1:T(8,128)(2,1)S(1)}, bf16[96,3,256]{2,0,1:T(8,128)(2,1)}, u32[]{:S(2)}) copy-start(bf16[96,3,256]{2,0,1:T(8,128)(2,1)} %param.25) | copy-start | bytes 442372
  25.7 1.4 %copy-start.6 = (f32[4]{0:T(128)S(1)}, f32[4]{0:T(128)}, u32[]{:S(2)}) copy-start(f32[4]{0:T(128)} %param.30) | copy-start | bytes 52
  25.7 1.4 %copy-start.7 = (f32[4]{0:T(128)S(1)}, f32[4]{0:T(128)}, u32[]{:S(2)}) copy-start(f32[4]{0:T(128)} %param.29) | copy-start | bytes 52
  25.7 3.3 %copy-start.5 = (f32[4]{0:T(128)S(1)}, f32[4]{0:T(128)}, u32[]{:S(2)}) copy-start(f32[4]{0:T(128)} %param.31) | copy-start | bytes 52
  29.7 15.2 %copy-start.3 = (bf16[2688]{0:T(1024)(128)(2,1)S(1)}, bf16[2688]{0:T(1024)(128)(2,1)}, u32[]{:S(2)}) copy-start(bf16[2688]{0:T(1024)(128)(2,1)} %param.35) | copy-start | bytes 16132
  29.7 15.8 %copy-start.8 = (bf16[256]{0:T(256)(128)(2,1)S(1)}, bf16[256]{0:T(256)(128)(2,1)}, u32[]{:S(2)}) copy-start(bf16[256]{0:T(256)(128)(2,1)} %param.32) | copy-start | bytes 1540

commit v3 on v2

--- a/solution.py
+++ b/solution.py
@@ -208,7 +208,7 @@
     values = full[...]
     mean = jnp.mean(values * values, axis=0, keepdims=True)
     scaled = (values * lax.rsqrt(mean + EPSILON)).T
-    normed = (scaled * gain[...].astype(F32)).astype(BF16)
+    normed = (scaled * gain[...].astype(F32)[None]).astype(BF16)
     normed_out[...] = normed
     load.wait()
     raw = jnp.dot(normed, weights[...], preferred_element_type=F32).astype(BF16).astype(F32)
@@ -273,19 +273,51 @@
 
 
 def state_kernel(
-    rows, heads, decay, state, driven, inputs, gates, skips, in_maps, out_maps, new_state, gated
+    rows,
+    heads,
+    both,
+    window,
+    taps,
+    step_raw,
+    step_bias,
+    decay_log,
+    skip_gain,
+    state,
+    in_maps,
+    out_maps,
+    new_state,
+    gated,
 ):
-    base = pl.program_id(0) * rows
-    columns = driven[...].T
+    inner = heads * HEAD_DIM
+    head_ids = lax.broadcasted_iota(jnp.int32, (1, inner), 1) // HEAD_DIM
+
+    def spread(ref):
+        wide = jnp.zeros((1, inner), F32)
+        for h in range(heads):
+            wide = jnp.where(head_ids == h, ref[h], wide)
+        return wide
+
+    kernel = taps[...].astype(F32)
+    mixed = both[:, inner:].astype(F32) * kernel[3:4]
+    for k in range(3):
+        mixed = mixed + window[k].astype(F32) * kernel[k : k + 1]
+    inputs = (mixed * jax.nn.sigmoid(mixed)).astype(BF16).astype(F32)
+    raw = step_raw[...].astype(F32)
+    steps = jnp.zeros((rows, inner), F32)
+    for h in range(heads):
+        steps = jnp.where(head_ids == h, raw[:, h : h + 1], steps)
+    steps = jax.nn.softplus(steps + spread(step_bias))
+    decays = jnp.exp(-jnp.exp(spread(decay_log)) * steps).T
+    columns = (steps * inputs).T
     readers = out_maps[...].astype(BF16)
-    row_ids = lax.broadcasted_iota(jnp.int32, (rows, heads * HEAD_DIM), 0)
-    total = jnp.zeros((rows, heads * HEAD_DIM), F32)
+    row_ids = lax.broadcasted_iota(jnp.int32, (rows, inner), 0)
+    total = jnp.zeros((rows, inner), F32)
     for j in range(rows):
         maps = in_maps[j : j + 1, :]
         parts = []
         for h in range(heads):
-            column = columns[h * HEAD_DIM : (h + 1) * HEAD_DIM, j : j + 1]
-            fresh = decay[(base + j) * heads + h] * state[j, h] + column * maps
+            part = slice(h * HEAD_DIM, (h + 1) * HEAD_DIM)
+            fresh = decays[part, j : j + 1] * state[j, h] + columns[part, j : j + 1] * maps
             new_state[j, h] = fresh
             parts.append(fresh.astype(BF16))
         block = jnp.concatenate(parts, axis=0)
@@ -293,8 +325,8 @@
             readers, block, (((1,), (1,)), ((), ())), preferred_element_type=F32
         )
         total = jnp.where(row_ids == j, found, total)
-    readout = total + skips[...] * inputs[...]
-    gate = gates[...].astype(F32)
+    readout = total + spread(skip_gain) * inputs
+    gate = both[:, :inner].astype(F32)
     gated[...] = readout * (gate * jax.nn.sigmoid(gate))
 
 
@@ -356,7 +388,7 @@
 
     for k in range(1, partners):
         partner_copy(k).start()
-    weighted = (values * gated_gain[...].astype(F32)).astype(BF16)
+    weighted = (values * gated_gain[...].astype(F32)[None]).astype(BF16)
     mixed = jnp.dot(weighted, proj_out[...], preferred_element_type=F32)
     total = own_squares
     for k in range(1, partners):
@@ -368,7 +400,7 @@
         outgoing[i] = terms[i * width : (i + 1) * width, :].astype(BF16)
 
     def prepare():
-        gain = moe_gain[...].astype(F32)
+        gain = moe_gain[...].astype(F32)[None]
         gains[...] = jnp.broadcast_to(gain, (seqs, gain.shape[1])).T
         folded = router[...].astype(F32) * gain
         high = folded.astype(BF16)
@@ -408,11 +440,6 @@
         outgoing[i] = (block * weight).astype(BF16)
     reduced = reduce_all(n, me, outgoing, bufs[half:])
     result[...] = (hidden_own[...].astype(F32) + reduced).astype(BF16)
-
-
-def convolve(window, fresh, kernel):
-    stacked = jnp.concatenate([window, fresh[:, None, :]], axis=1).astype(F32)
-    return jax.nn.silu(jnp.sum(stacked * kernel.astype(F32)[None], axis=1)).astype(BF16)
 
 
 def vmem(count):
@@ -474,21 +501,22 @@
             DMA((readers,)),
             DMA((slots,)),
         ],
-        compiler_params=pltpu.CompilerParams(collective_id=0, has_side_effects=True),
+        compiler_params=pltpu.CompilerParams(
+            collective_id=0, has_side_effects=True, vmem_limit_bytes=54 << 20
+        ),
+        cost_estimate=pl.CostEstimate(
+            flops=2 * seqs * full_width * cols, bytes_accessed=40 << 20, transcendentals=0
+        ),
         name="gather_tokens",
-    )(tokens.T, mix_gain[None], proj_maps, window_maps.transpose(1, 0, 2), kernel_maps)
+    )(tokens.T, mix_gain, proj_maps, window_maps.transpose(1, 0, 2), kernel_maps)
     both = jnp.dot(
         normed, proj_inner.reshape(full_width, 2 * inner), preferred_element_type=F32
     ).astype(BF16)
     step_raw = jnp.dot(normed, proj_step, preferred_element_type=F32).astype(BF16)
-    conv_inner = convolve(window_inner, both[:, inner:], kernel_inner).astype(F32)
-    step_size = jax.nn.softplus(step_raw.astype(F32) + step_bias)
-    decay = jnp.exp(-jnp.exp(decay_log) * step_size)
-    driven = jnp.repeat(step_size, HEAD_DIM, axis=1) * conv_inner
-    rows = 8
-    skips = jnp.repeat(skip_gain, HEAD_DIM)[None]
+    rows = 16
     by_row = lambda i: (i, 0)
     by_state = lambda i: (i, 0, 0, 0)
+    scalars = pl.BlockSpec(memory_space=pltpu.SMEM)
     new_state, gated = pl.pallas_call(
         functools.partial(state_kernel, rows, heads),
         grid=(seqs // rows,),
@@ -497,12 +525,14 @@
             jax.ShapeDtypeStruct((seqs, inner), F32),
         ),
         in_specs=[
-            pl.BlockSpec(memory_space=pltpu.SMEM),
+            pl.BlockSpec((rows, 2 * inner), by_row),
+            pl.BlockSpec((3, rows, inner), lambda i: (0, i, 0)),
+            pl.BlockSpec(kernel_inner.shape, lambda i: (0, 0)),
+            pl.BlockSpec((rows, heads), by_row),
+            scalars,
+            scalars,
+            scalars,
             pl.BlockSpec((rows, heads, HEAD_DIM, STATE), by_state),
-            pl.BlockSpec((rows, inner), by_row),
-            pl.BlockSpec((rows, inner), by_row),
-            pl.BlockSpec((rows, inner), by_row),
-            pl.BlockSpec((1, inner), lambda i: (0, 0)),
             pl.BlockSpec((rows, STATE), by_row),
             pl.BlockSpec((rows, STATE), by_row),
         ],
@@ -510,14 +540,17 @@
             pl.BlockSpec((rows, heads, HEAD_DIM, STATE), by_state),
             pl.BlockSpec((rows, inner), by_row),
         ),
+        compiler_params=pltpu.CompilerParams(vmem_limit_bytes=54 << 20),
         name="update_state",
     )(
-        decay.reshape(-1),
+        both,
+        window_inner.transpose(1, 0, 2),
+        kernel_inner,
+        step_raw,
+        step_bias,
+        decay_log,
+        skip_gain,
         ssm_state,
-        driven,
-        conv_inner,
-        both[:, :inner].astype(F32),
-        skips,
         in_maps,
         out_maps,
     )
@@ -562,14 +595,16 @@
             DMA((n,)),
         ]
         + reduce_bufs * 2,
-        compiler_params=pltpu.CompilerParams(collective_id=1, has_side_effects=True),
+        compiler_params=pltpu.CompilerParams(
+            collective_id=1, has_side_effects=True, vmem_limit_bytes=60 << 20
+        ),
         name="mix_and_serve",
     )(
         gated,
-        gated_gain[None],
+        gated_gain,
         proj_out,
         tokens.T,
-        moe_gain[None],
+        moe_gain,
         router_weight.T,
         expert_ids.T,
         expert_up.swapaxes(1, 2),

time: 91.8 us -> 87 us (0.948)
  local copies, waits for them, and re-layouts: 7.89 us -> 4.49 us
  matrix products: 0.85 us -> 2.46 us
  other arithmetic: 1.41 us -> 0 us
  Pallas kernels: 80.2 us -> 79 us
    broadcast_in_dim x5 -> x0, local copies, waits for them, and re-layouts: 2.59 us -> none  [the longest x1 1.3 us: local(): mix_gain[None]]
    convert_element_type x3 -> x0, other arithmetic: 1.37 us -> none  [the longest x1 0.7 us: local(): convolve(window_inner, both[:, inner:], kernel_inner).astype(F32)]
    pallas_call x1, Pallas kernels: 15.2 us -> 13.9 us  [local(): pl.pallas_call(functools.partial(state_kernel, rows, heads), grid=(seqs /...]
    dot_general x1, matrix products: 0.27 us -> 1.25 us  [local(): jnp.dot(normed, proj_step, preferred_element_type=F32).astype(BF16)]
    unnamed x20 -> x6, local copies, waits for them, and re-layouts: 3.75 us -> 3.71 us
where the time goes in v3:
time: 87 us; the launch traced here: 86.6 us
  Pallas kernels  79 us (91%)
  local copies, waits for them, and re-layouts  4.49 us (5%)
  matrix products  2.46 us (3%)
    pallas_call x1, Pallas kernels, local(): pl.pallas_call(functools.partial(expert_kernel, n, readers), out_shape=ja...  43.7 us
    pallas_call x1, Pallas kernels, local(): pl.pallas_call(functools.partial(gather_kernel, n, heads), out_shape=(jax...  21.4 us
    pallas_call x1, Pallas kernels, local(): pl.pallas_call(functools.partial(state_kernel, rows, heads), grid=(seqs /...  13.9 us
    unnamed x6, local copies, waits for them, and re-layouts  3.71 us

profile of v3, /device:TPU:0, one launch (start us, length us, event | category | flops | bytes accessed | tf_op | source)
XLA Modules:
  0.0 86.6 jit_solution(6426018385889034435)
XLA Ops:
  0.6 0.0 copy-start
  0.6 21.4 %gather_tokens.1 = (bf16[96,2688]{1,0:T(8,128)(2,1)}, f32[96,128]{1,0:T(8,128)}, f32[96,128]{1,0:T(8,128)}) custom-call(bf16[168,96]{1,0:T(8,128)(2,1)} %bitcast.17, bf16[2688]{0:T(1024)(128)(2,1)} %gain.1, bf16[2688,128]{1,0:T(8,128)(2,1)} %weights_hbm.1, bf16[3,96,128]{2,1,0:T(8,128)(2,1)} %bitcast.21, bf16[4,128]{1,0:T(4,128)(2,1)} %taps.2), custom_call_target="tpu_custom_call" | custom-call | flops 66060288 | bytes 41943040 | tf_op jit(solution)/shard_map/gather_tokens/pallas_call | solution.py:483
  22.1 0.0 copy-done
  22.1 1.2 %convolution_convert_fusion.1 = bf16[96,4]{0,1:T(4,128)(2,1)S(1)} fusion(bf16[96,2688]{1,0:T(8,128)(2,1)} %get-tuple-element.7, bf16[2688,4]{0,1:T(4,128)(2,1)S(1)} %copy-done), kind=kOutput, calls=%fused_computation.1 | convolution fusion | flops 2064768 | bytes 538368 | tf_op jit(solution)/shard_map/dot_general | solution.py:515
  23.4 0.8 copy.23.step_raw
  24.1 0.0 copy-start.1
  24.1 2.3 %copy.24 = bf16[336,8,2,256]{3,1,2,0:T(8,128)(2,1)S(1)} copy(bf16[336,8,2,256]{3,2,1,0:T(2,128)(2,1)} %bitcast.15) | data formatting | bytes 5505024
  26.4 0.0 copy-done.1
  26.5 1.2 %convolution_convert_fusion.both = bf16[96,512]{1,0:T(8,128)(2,1)} fusion(bf16[96,2688]{1,0:T(8,128)(2,1)S(1)} %copy-done.1, bf16[2688,512]{1,0:T(8,128)(2,1)S(1)} %bitcast.13), kind=kOutput, calls=%fused_computation | convolution fusion | flops 264290304 | bytes 3366912 | tf_op jit(solution)/shard_map/dot_general | solution.py:512
  27.7 13.9 %update_state.1 = (f32[96,4,64,128]{3,2,1,0:T(8,128)}, f32[96,256]{1,0:T(8,128)}) custom-call(bf16[96,512]{1,0:T(8,128)(2,1)} %convolution_convert_fusion.both, bf16[3,96,256]{2,1,0:T(8,128)(2,1)} %bitcast.19, bf16[4,256]{1,0:T(4,128)(2,1)} %taps.3, bf16[96,4]{1,0:T(8,128)(2,1)} %copy.23.step_raw, f32[4]{0:T(128)} %step_bias.1, f32[4]{0:T(128)} %decay_log.1, ...), custom_call_target="tpu_custom_call" | custom-call | tf_op jit(solution)/shard_map/update_state/pallas_call | solution.py:520
  41.5 43.7 %mix_and_serve.1 = bf16[168,96]{1,0:T(8,128)(2,1)} custom-call(f32[96,256]{1,0:T(8,128)} %get-tuple-element.10.gated, bf16[256]{0:T(256)(128)(2,1)} %gated_gain.1, bf16[256,2688]{1,0:T(8,128)(2,1)} %proj_out.1, bf16[168,96]{1,0:T(8,128)(2,1)} %bitcast.18, bf16[2688]{0:T(1024)(128)(2,1)} %moe_gain.1, bf16[16,2688]{1,0:T(8,128)(2,1)} %bitcast.20, ...), custom_call_target="tpu_custom_call" | custom-call | tf_op jit(solution)/shard_map/mix_and_serve/pallas_call | solution.py:574
  85.2 1.4 %copy.26 = bf16[96,168]{0,1:T(8,128)(2,1)} copy(bf16[96,168]{0,1:T(8,128)(2,1)} %bitcast.16) | data formatting | bytes 64512
Async XLA Ops:
  0.6 21.5 %copy-start = (bf16[2688,4]{0,1:T(4,128)(2,1)S(1)}, bf16[2688,4]{0,1:T(4,128)(2,1)}, u32[]{:S(2)}) copy-start(bf16[2688,4]{0,1:T(4,128)(2,1)} %param.24) | copy-start | bytes 64516
  24.1 2.3 %copy-start.1 = (bf16[96,2688]{1,0:T(8,128)(2,1)S(1)}, bf16[96,2688]{1,0:T(8,128)(2,1)}, u32[]{:S(2)}) copy-start(bf16[96,2688]{1,0:T(8,128)(2,1)} %get-tuple-element.7) | copy-start | bytes 1548292

commit v4 on v3

--- a/solution.py
+++ b/solution.py
@@ -173,6 +173,36 @@
     return total
 
 
+LANES = 128
+
+
+def packed_shape(width, seqs):
+    gap = LANES - seqs
+    if gap <= 0 or seqs % gap:
+        return width, 0, 0
+    chunks = seqs // gap
+    rest = width // (chunks + 1) // 8 * 8
+    return width - rest, rest, gap
+
+
+def pack_into(target, source):
+    width, seqs = source.shape
+    kept, rest, gap = packed_shape(width, seqs)
+    target[:, :seqs] = source[:kept, :]
+    if rest:
+        for c in range(seqs // gap):
+            target[c * rest : (c + 1) * rest, seqs:] = source[kept:, c * gap : (c + 1) * gap]
+
+
+def unpack_into(target, value):
+    width, seqs = target.shape
+    kept, rest, gap = packed_shape(width, seqs)
+    target[:kept, :] = value[:, :seqs]
+    if rest:
+        for c in range(seqs // gap):
+            target[kept:, c * gap : (c + 1) * gap] = value[c * rest : (c + 1) * rest, seqs:]
+
+
 def gather_kernel(
     n,
     local_heads,
@@ -181,11 +211,15 @@
     weights_hbm,
     window,
     taps,
+    step_weights,
     normed_out,
     in_out,
     out_out,
+    step_out,
     landing,
     full,
+    packing,
+    own,
     weights,
     mapped,
     arrived,
@@ -201,10 +235,14 @@
     load = pltpu.make_async_copy(weights_hbm, weights, weight_sem)
     load.start()
     greet_all(n, me)
+    full[:width, :] = tokens[...].astype(F32)
+    packing[...] = jnp.zeros_like(packing)
+    pack_into(packing, full.at[:width, :])
+    own[...] = packing[...].astype(BF16)
     await_all(n)
-    gather_all(n, me, tokens, landing, send_sems, recv_sems)
+    gather_all(n, me, own, landing, send_sems, recv_sems)
     for i in range(n):
-        full[i * width : (i + 1) * width, :] = landing[i].astype(F32)
+        unpack_into(full.at[i * width : (i + 1) * width, :], landing[i].astype(F32))
     values = full[...]
     mean = jnp.mean(values * values, axis=0, keepdims=True)
     scaled = (values * lax.rsqrt(mean + EPSILON)).T
@@ -246,6 +284,9 @@
         def _():
             arrived[own_slot] = mapped[...]
 
+    step_out[...] = lax.dot_general(
+        normed, step_weights[...], (((1,), (1,)), ((), ())), preferred_element_type=F32
+    ).astype(BF16)
     group = me // readers
     for slot in range(2 * per_group):
         origin = (slot // per_group) * half + group * per_group + slot % per_group
@@ -349,6 +390,8 @@
     gains,
     router_hi,
     router_lo,
+    packing,
+    own,
     outgoing,
     hidden_own,
     hidden_all,
@@ -371,6 +414,10 @@
     values = gated[...]
     own_squares = jnp.sum(values * values, axis=1, keepdims=True)
     squares[...] = jnp.broadcast_to(own_squares, squares.shape)
+    packing[...] = jnp.zeros_like(packing)
+    own[...] = jnp.zeros_like(own)
+    terms[:width, :] = tokens[...].astype(F32)
+    pack_into(own, terms.at[:width, :])
     await_all(n)
     first = (me // partners) * partners
     place = lax.rem(me, partners)
@@ -397,7 +444,8 @@
     channels = values.shape[1] * partners
     terms[...] = (mixed * lax.rsqrt(total / channels + EPSILON)).T
     for i in range(n):
-        outgoing[i] = terms[i * width : (i + 1) * width, :].astype(BF16)
+        pack_into(packing.at[i], terms.at[i * width : (i + 1) * width, :])
+        outgoing[i] = packing[i].astype(BF16)
 
     def prepare():
         gain = moe_gain[...].astype(F32)[None]
@@ -409,10 +457,10 @@
 
     half = len(bufs) // 2
     reduced = reduce_all(n, me, outgoing, bufs[:half], prepare)
-    hidden_own[...] = (tokens[...].astype(F32) + reduced).astype(BF16)
+    hidden_own[...] = (own[...] + reduced).astype(BF16)
     gather_all(n, me, hidden_own, hidden_all, hid_send, hid_recv)
     for i in range(n):
-        terms[i * width : (i + 1) * width, :] = hidden_all[i].astype(F32)
+        unpack_into(terms.at[i * width : (i + 1) * width, :], hidden_all[i].astype(F32))
     values = terms[...]
     mean = jnp.mean(values * values, axis=0, keepdims=True)
     moe_scale = lax.rsqrt(mean + EPSILON)
@@ -434,12 +482,13 @@
     active = jnp.square(jnp.maximum(units, 0.0)).T.astype(BF16)
     load_down.wait()
     served = jnp.dot(active, down[0], preferred_element_type=F32)
-    terms[...] = served.T
+    terms[...] = served.T.astype(BF16).astype(F32) * weight
     for i in range(n):
-        block = terms[i * width : (i + 1) * width, :].astype(BF16).astype(F32)
-        outgoing[i] = (block * weight).astype(BF16)
+        pack_into(packing.at[i], terms.at[i * width : (i + 1) * width, :])
+        outgoing[i] = packing[i].astype(BF16)
     reduced = reduce_all(n, me, outgoing, bufs[half:])
-    result[...] = (hidden_own[...].astype(F32) + reduced).astype(BF16)
+    unpack_into(terms.at[:width, :], hidden_own[...].astype(F32) + reduced)
+    result[...] = terms[:width, :].astype(BF16)
 
 
 def vmem(count):
@@ -480,18 +529,22 @@
     heads = proj_step.shape[1]
     readers = HEADS // GROUPS // heads
     slots = 2 * (STATE // cols)
-    normed, in_maps, out_maps = pl.pallas_call(
+    kept = packed_shape(width, seqs)[0]
+    normed, in_maps, out_maps, step_raw = pl.pallas_call(
         functools.partial(gather_kernel, n, heads),
         out_shape=(
             jax.ShapeDtypeStruct((seqs, full_width), BF16),
             jax.ShapeDtypeStruct((seqs, STATE), F32),
             jax.ShapeDtypeStruct((seqs, STATE), F32),
+            jax.ShapeDtypeStruct((seqs, heads), BF16),
         ),
-        in_specs=vmem(2) + [ANY] + vmem(2),
-        out_specs=tuple(vmem(3)),
+        in_specs=vmem(2) + [ANY] + vmem(3),
+        out_specs=tuple(vmem(4)),
         scratch_shapes=[
-            pltpu.VMEM((n, width, seqs), BF16),
+            pltpu.VMEM((n, kept, LANES), BF16),
             pltpu.VMEM((full_width, seqs), F32),
+            pltpu.VMEM((kept, LANES), F32),
+            pltpu.VMEM((kept, LANES), BF16),
             pltpu.VMEM((full_width, cols), BF16),
             pltpu.VMEM((seqs, cols), BF16),
             pltpu.VMEM((slots, seqs, cols), BF16),
@@ -508,11 +561,10 @@
             flops=2 * seqs * full_width * cols, bytes_accessed=40 << 20, transcendentals=0
         ),
         name="gather_tokens",
-    )(tokens.T, mix_gain, proj_maps, window_maps.transpose(1, 0, 2), kernel_maps)
+    )(tokens.T, mix_gain, proj_maps, window_maps.transpose(1, 0, 2), kernel_maps, proj_step.T)
     both = jnp.dot(
         normed, proj_inner.reshape(full_width, 2 * inner), preferred_element_type=F32
     ).astype(BF16)
-    step_raw = jnp.dot(normed, proj_step, preferred_element_type=F32).astype(BF16)
     rows = 16
     by_row = lambda i: (i, 0)
     by_state = lambda i: (i, 0, 0, 0)
@@ -557,7 +609,7 @@
     lines = n // 4
 
     def piece(count):
-        return pltpu.VMEM((count, width, seqs), BF16)
+        return pltpu.VMEM((count, kept, LANES), BF16)
 
     reduce_bufs = [
         piece(2 * lines),
@@ -583,8 +635,10 @@
             pltpu.VMEM((full_width, seqs), F32),
             pltpu.VMEM((router_weight.shape[1], full_width), BF16),
             pltpu.VMEM((router_weight.shape[1], full_width), BF16),
+            pltpu.VMEM((n, kept, LANES), F32),
+            pltpu.VMEM((kept, LANES), F32),
             piece(n),
-            pltpu.VMEM((width, seqs), BF16),
+            pltpu.VMEM((kept, LANES), BF16),
             piece(n),
             pltpu.VMEM((seqs, 128), F32),
             pltpu.VMEM((readers - 1, seqs, 128), F32),

time: 87 us -> 83 us (0.954)
  Pallas kernels: 79 us -> 77 us
  matrix products: 2.46 us -> 1.21 us
    pallas_call x1, Pallas kernels: 43.7 us -> 42.3 us  [local(): pl.pallas_call(functools.partial(expert_kernel, n, readers), out_shape=ja...]
    dot_general x1 -> x0, matrix products: 1.25 us -> none  [local(): jnp.dot(normed, proj_step, preferred_element_type=F32).astype(BF16)]
    unnamed x6 -> x4, local copies, waits for them, and re-layouts: 3.71 us -> 3.7 us
where the time goes in v4:
time: 83 us; the launch traced here: 82.6 us
  Pallas kernels  77 us (93%)
  local copies, waits for them, and re-layouts  3.7 us (4%)
  matrix products  1.21 us (1%)
    pallas_call x1, Pallas kernels, local(): pl.pallas_call(functools.partial(expert_kernel, n, readers), out_shape=ja...  42.3 us
    pallas_call x1, Pallas kernels, local(): pl.pallas_call(functools.partial(gather_kernel, n, heads), out_shape=(jax...  20.8 us
    pallas_call x1, Pallas kernels, local(): pl.pallas_call(functools.partial(state_kernel, rows, heads), grid=(seqs /...  13.9 us
    unnamed x4, local copies, waits for them, and re-layouts  3.7 us

profile of v4, /device:TPU:0, one launch (start us, length us, event | category | flops | bytes accessed | tf_op | source)
XLA Modules:
  0.0 82.6 jit_solution(5654770988122193748)
XLA Ops:
  0.6 20.8 %gather_tokens.1 = (bf16[96,2688]{1,0:T(8,128)(2,1)}, f32[96,128]{1,0:T(8,128)}, f32[96,128]{1,0:T(8,128)}, bf16[96,4]{1,0:T(8,128)(2,1)}) custom-call(bf16[168,96]{1,0:T(8,128)(2,1)} %bitcast.16, bf16[2688]{0:T(1024)(128)(2,1)} %gain.1, bf16[2688,128]{1,0:T(8,128)(2,1)} %weights_hbm.1, bf16[3,96,128]{2,1,0:T(8,128)(2,1)} %bitcast.20, bf16[4,128]{1,0:T(4,128)(2,1)} %taps.2, ...), custom_call_target="tpu_custom_call" | custom-call | flops 66060288 | bytes 41943040 | tf_op jit(solution)/shard_map/gather_tokens/pallas_call | solution.py:533
  21.4 0.0 copy-start
  21.5 2.3 %copy.22 = bf16[336,8,2,256]{3,1,2,0:T(8,128)(2,1)S(1)} copy(bf16[336,8,2,256]{3,2,1,0:T(2,128)(2,1)} %bitcast.14) | data formatting | bytes 5505024
  23.7 0.0 copy-done
  23.8 1.2 %convolution_convert_fusion.both = bf16[96,512]{1,0:T(8,128)(2,1)} fusion(bf16[96,2688]{1,0:T(8,128)(2,1)S(1)} %copy-done, bf16[2688,512]{1,0:T(8,128)(2,1)S(1)} %bitcast.12), kind=kOutput, calls=%fused_computation | convolution fusion | flops 264290304 | bytes 3366912 | tf_op jit(solution)/shard_map/dot_general | solution.py:565
  25.0 13.9 %update_state.1 = (f32[96,4,64,128]{3,2,1,0:T(8,128)}, f32[96,256]{1,0:T(8,128)}) custom-call(bf16[96,512]{1,0:T(8,128)(2,1)} %convolution_convert_fusion.both, bf16[3,96,256]{2,1,0:T(8,128)(2,1)} %bitcast.18, bf16[4,256]{1,0:T(4,128)(2,1)} %taps.3, bf16[96,4]{1,0:T(8,128)(2,1)} %get-tuple-element.9.step_raw, f32[4]{0:T(128)} %step_bias.1, f32[4]{0:T(128)} %decay_log.1, ...), custom_call_target="tpu_custom_call" | custom-call | tf_op jit(solution)/shard_map/update_state/pallas_call | solution.py:572
  38.8 42.3 %mix_and_serve.1 = bf16[168,96]{1,0:T(8,128)(2,1)} custom-call(f32[96,256]{1,0:T(8,128)} %get-tuple-element.12.gated, bf16[256]{0:T(256)(128)(2,1)} %gated_gain.1, bf16[256,2688]{1,0:T(8,128)(2,1)} %proj_out.1, bf16[168,96]{1,0:T(8,128)(2,1)} %bitcast.17, bf16[2688]{0:T(1024)(128)(2,1)} %moe_gain.1, bf16[16,2688]{1,0:T(8,128)(2,1)} %bitcast.19, ...), custom_call_target="tpu_custom_call" | custom-call | tf_op jit(solution)/shard_map/mix_and_serve/pallas_call | solution.py:626
  81.2 1.4 %copy.24 = bf16[96,168]{0,1:T(8,128)(2,1)} copy(bf16[96,168]{0,1:T(8,128)(2,1)} %bitcast.15) | data formatting | bytes 64512
Async XLA Ops:
  21.4 2.3 %copy-start = (bf16[96,2688]{1,0:T(8,128)(2,1)S(1)}, bf16[96,2688]{1,0:T(8,128)(2,1)}, u32[]{:S(2)}) copy-start(bf16[96,2688]{1,0:T(8,128)(2,1)} %get-tuple-element.8) | copy-start | bytes 1548292
